TPU v7x, 1024 devices: a whole 8x8x8 slice. The times are simulated.
1024 devices in a mesh: expert: 64 (over x, y), hidden: 16 (over z, core).
Axes of the slice: x: 8, y: 8, z: 8, core: 2. Of those that a mesh axis runs over, the one named last changes fastest.
Arguments:
- tokens: bfloat16 [16, 128, 2048], P('hidden', 'expert'), may hold values from -6 to 6
- grad_out: bfloat16 [16, 128, 2048], P('hidden', 'expert'), may hold values from -6 to 6
- expert_ids: int32 [16, 128, 8], P('hidden', 'expert'), may hold values from 0 to 63, all different within a row; in each aligned block of 128 rows (0 to 127, 128 to 255, ..., all dimensions but the last counted through in order) at most 32 rows name the same one
- router_logits: float32 [16, 128, 8], P('hidden', 'expert'), may hold values from -4 to 4
- w_gate: bfloat16 [64, 2048, 1536], P('expert', None, 'hidden'), may hold values from -0.125 to 0.125
- w_up: bfloat16 [64, 2048, 1536], P('expert', None, 'hidden'), may hold values from -0.125 to 0.125
- w_down: bfloat16 [64, 1536, 2048], P('expert', 'hidden'), may hold values from -0.15625 to 0.15625
Outputs:
- grad_in: float32 [16, 128, 2048], P('hidden', 'expert')
- grad_logits: float32 [16, 128, 8], P('hidden', 'expert')
- grad_gate: float32 [64, 2048, 1536], P('expert', None, 'hidden')
- grad_up: float32 [64, 2048, 1536], P('expert', None, 'hidden')
- grad_down: float32 [64, 1536, 2048], P('expert', 'hidden')
Inputs may be any that keep to these rules, and one draw needn't show every extreme that they name: `expert_ids`: each token names 8 different experts. Among the tokens of one hidden index no expert is named more than 32 times, a bound that some block reaches.
All inputs are finite; a program needn't handle non-finite values.
Results may differ from a plain program's by a relative error of at most 0.0041.
Values may be sent and summed in bfloat16 or wider, within the bound.
A program may use at most 32 MiB of HBM per device.

v0:
```python
import jax
import jax.numpy as jnp
from jax import lax
from jax.sharding import PartitionSpec as P

TOP = 8


def expert_core(x_rows, grad_rows, gate_col, gate_weight, up_weight, down_weight):
    pre_gate = jnp.dot(x_rows, gate_weight, preferred_element_type=jnp.float32)
    pre_up = jnp.dot(x_rows, up_weight, preferred_element_type=jnp.float32)
    back_grad = lax.dot_general(
        grad_rows, down_weight, (((1,), (1,)), ((), ())), preferred_element_type=jnp.float32
    )
    sigmoid_gate = jax.nn.sigmoid(pre_gate)
    silu_gate = pre_gate * sigmoid_gate
    active = silu_gate * pre_up
    gate_grad = jnp.sum(active * back_grad, axis=-1)
    weight = gate_col.astype(jnp.float32)
    scaled = (weight * active).astype(jnp.bfloat16)
    weighted_back = weight * back_grad
    d_gate_pre = (
        weighted_back * pre_up * sigmoid_gate * (1.0 + pre_gate * (1.0 - sigmoid_gate))
    ).astype(jnp.bfloat16)
    d_up_pre = (weighted_back * silu_gate).astype(jnp.bfloat16)
    sum_gate = lax.dot_general(
        x_rows, d_gate_pre, (((0,), (0,)), ((), ())), preferred_element_type=jnp.float32
    )
    sum_up = lax.dot_general(
        x_rows, d_up_pre, (((0,), (0,)), ((), ())), preferred_element_type=jnp.float32
    )
    sum_down = lax.dot_general(
        scaled, grad_rows, (((0,), (0,)), ((), ())), preferred_element_type=jnp.float32
    )
    return (gate_grad, d_gate_pre, d_up_pre, sum_gate, sum_up, sum_down)


def project_back(d_gate_pre, d_up_pre, gate_weight, up_weight):
    row_grad = lax.dot_general(
        d_gate_pre, gate_weight, (((1,), (1,)), ((), ())), preferred_element_type=jnp.float32
    )
    return row_grad + lax.dot_general(
        d_up_pre, up_weight, (((1,), (1,)), ((), ())), preferred_element_type=jnp.float32
    )


def on_device(tokens, grad_out, expert_ids, router_logits, w_gate, w_up, w_down):
    highest = lax.Precision.HIGHEST
    tok_dev = tokens.shape[1]
    peers = lax.axis_size("expert")
    mine = lax.axis_index("expert")
    row_cap = min(2 * tok_dev * TOP, tok_dev * peers)
    raised = jnp.exp(router_logits[0])
    gate_probs = raised / jnp.sum(raised, axis=-1, keepdims=True)
    gate_rows = gate_probs.astype(jnp.bfloat16)
    expert_range = jnp.arange(peers, dtype=jnp.int32)
    chosen = expert_ids[0][:, :, None] == expert_range[None, None, :]
    per_peer = jnp.sum(
        jnp.where(chosen, gate_rows.astype(jnp.float32)[:, :, None], jnp.float32(0.0)), axis=1
    )
    gate_table = per_peer.astype(jnp.bfloat16)
    got_x, got_grad, got_table = (
        lax.all_gather(tokens, "expert", axis=1, tiled=True),
        lax.all_gather(grad_out, "expert", axis=1, tiled=True),
        lax.all_gather(gate_table[None], "expert", axis=1, tiled=True),
    )
    all_x = got_x[0]
    all_grad = got_grad[0]
    column = jnp.sum(
        jnp.where(
            expert_range[None, :] == mine, got_table[0].astype(jnp.float32), jnp.float32(0.0)
        ),
        axis=-1,
    )
    picked = column > 0.0
    row_order = jnp.cumsum(picked.astype(jnp.int32)) - 1
    placing = (row_order[None, :] == jnp.arange(row_cap, dtype=jnp.int32)[:, None]) & picked[
        None, :
    ]
    placing_half = placing.astype(jnp.bfloat16)
    placing_full = placing.astype(jnp.float32)
    x_rows = jnp.dot(placing_half, all_x, preferred_element_type=jnp.float32).astype(jnp.bfloat16)
    grad_rows = jnp.dot(placing_half, all_grad, preferred_element_type=jnp.float32).astype(
        jnp.bfloat16
    )
    gate_col = jnp.dot(placing_full, column, precision=highest).astype(jnp.bfloat16)[:, None]
    gate_weight = w_gate[0]
    up_weight = w_up[0]
    down_weight = w_down[0]
    cycle_x, cycle_grad, cycle_gate = (
        lax.all_gather(x_rows, "hidden", axis=0, tiled=True),
        lax.all_gather(grad_rows, "hidden", axis=0, tiled=True),
        lax.all_gather(gate_col, "hidden", axis=0, tiled=True),
    )
    gate_part, gate_pre_all, up_pre_all, sum_gate, sum_up, sum_down = expert_core(
        cycle_x, cycle_grad, cycle_gate, gate_weight, up_weight, down_weight
    )
    row_part = project_back(gate_pre_all, up_pre_all, gate_weight, up_weight)
    own_rows, own_gate = (
        lax.psum_scatter(row_part, "hidden", scatter_dimension=0, tiled=True),
        lax.psum_scatter(gate_part, "hidden", scatter_dimension=0, tiled=True),
    )
    dense = lax.dot_general(placing_full, own_rows, (((0,), (0,)), ((), ())), precision=highest)
    token_gate = lax.dot_general(
        placing_full, own_gate, (((0,), (0,)), ((), ())), precision=highest
    )
    gate_out = jnp.where(expert_range[None, :] == mine, token_gate[:, None], jnp.float32(0.0))
    summed, gate_sums = (
        lax.psum_scatter(dense[None], "expert", scatter_dimension=1, tiled=True),
        lax.psum_scatter(gate_out[None], "expert", scatter_dimension=1, tiled=True),
    )
    gate_grad = jnp.sum(jnp.where(chosen, gate_sums[0][:, None, :], jnp.float32(0.0)), axis=-1)
    grad_logits = gate_probs * (gate_grad - jnp.sum(gate_probs * gate_grad, axis=-1, keepdims=True))
    return (summed, grad_logits[None], sum_gate[None], sum_up[None], sum_down[None])


def solution(mesh):
    in_specs = (
        P("hidden", "expert", None),
        P("hidden", "expert", None),
        P("hidden", "expert", None),
        P("hidden", "expert", None),
        P("expert", None, "hidden"),
        P("expert", None, "hidden"),
        P("expert", "hidden", None),
    )
    out_specs = (
        P("hidden", "expert", None),
        P("hidden", "expert", None),
        P("expert", None, "hidden"),
        P("expert", None, "hidden"),
        P("expert", "hidden", None),
    )
    return jax.shard_map(
        on_device, mesh=mesh, in_specs=in_specs, out_specs=out_specs, check_vma=False
    )
```

profile of v0, /device:TPU:14, one launch (start us, length us, event | category | flops | bytes accessed | tf_op | source)
XLA Modules:
  0.0 693.5 jit_solution(7454320506488024764)
XLA Ops:
  7.2 0.0 copy-start
  7.2 0.0 all-gather.8.cloned.1.call-start
  7.3 0.8 exponential_reduce_fusion
  8.1 0.8 convert_convert_fusion
  8.8 0.7 copy.22
  9.5 0.8 select_reduce_fusion.1
  10.3 51.4 %all-gather.2 = bf16[64,2,64]{2,1,0:T(2,128)(2,1)S(1)} all-gather(bf16[1,2,64]{2,1,0:T(2,128)(2,1)S(1)} %bitcast.79), channel_id=2, replica_groups=mesh['expert'=64,'hidden'=16] {'expert'}, dimensions={0}, use_global_device_ids=true | all-gather | bytes 16640 | tf_op jit(solution)/shard_map/all_gather | solution.py:65
  61.7 0.1 fusion.17
  61.8 0.1 copy.20
  61.9 0.2 reduce-window.8
  62.1 0.1 add_reduce_fusion
  62.2 47.1 %all_gather.22 = bf16[1,128,2048]{2,0,1:T(2,128)(2,1)S(1)} all-gather(bf16[1,2,2048]{2,0,1:T(2,128)(2,1)S(1)} %copy.22), channel_id=1, replica_groups=mesh['expert'=64,'hidden'=16] {'expert'}, dimensions={1}, use_global_device_ids=true | all-gather | bytes 532480 | tf_op jit(solution)/shard_map/all_gather | solution.py:63
  109.3 1.1 convolution_convert_fusion
  110.4 0.0 all-gather.8.cloned.1.call-update
  110.4 0.0 all-gather.6.cloned.1.call-start
  110.5 0.0 copy-start.3
  110.5 49.7 %all_gather.20 = bf16[1,128,2048]{2,0,1:T(2,128)(2,1)S(1)} all-gather(bf16[1,2,2048]{2,0,1:T(2,128)(2,1)S(1)} %copy.21), channel_id=1, replica_groups=mesh['expert'=64,'hidden'=16] {'expert'}, dimensions={1}, use_global_device_ids=true | all-gather | bytes 532480 | tf_op jit(solution)/shard_map/all_gather | solution.py:64
  160.2 1.1 convolution_convert_fusion.1
  161.3 0.0 all-gather.6.cloned.1.call-update
  161.3 0.0 reduce-scatter.4.cloned.1.call-start
  161.4 1.4 fusion.36
  163.4 0.1 fusion
  163.5 0.2 dynamic-update-slice
  163.7 28.4 %all-reduce = bf16[512]{0:T(512)(128)(2,1)S(1)} all-reduce(bf16[512]{0:T(512)(128)(2,1)S(1)} %dynamic-update-slice), channel_id=3, replica_groups=mesh['expert'=64,'hidden'=16] {'hidden'}, use_global_device_ids=true, to_apply=%add | all-reduce | flops 512 | bytes 2048
  192.2 0.0 all-gather.8.cloned.1.call-done
  192.2 2.6 fusion.7
  194.8 0.8 fusion.10
  195.6 12.9 %all-gather.6.cloned.1.call-done = bf16[512,2048]{1,0:T(8,128)(2,1)} async-done(((bf16[32,2048]{1,0:T(8,128)(2,1)}), bf16[512,2048]{1,0:T(8,128)(2,1)}) %all-gather.6.cloned.1.call-update) | async-done | bytes 2097168 | tf_op jit(solution)/shard_map/all_gather | solution.py:92
  208.5 2.5 multiply_reduce_fusion
  210.9 0.7 fusion.5
  211.7 2.7 convolution_add_fusion
  214.3 0.0 reduce-scatter.4.cloned.1.call-update
  214.4 0.0 all-reduce.6.cloned.1.call-start
  214.4 1.3 dynamic-slice.1
  217.0 25.0 %all-reduce.2 = f32[512]{0:T(512)S(1)} all-reduce(f32[512]{0:T(512)S(1)} %get-tuple-element.7), channel_id=6, replica_groups=mesh['expert'=64,'hidden'=16] {'hidden'}, use_global_device_ids=true, to_apply=%region_7.8.clone | all-reduce | flops 512 | bytes 4096
  242.0 0.2 convolution_bitcast_fusion.4
  242.2 0.1 broadcast_select_fusion
  242.3 265.7 %all-reduce.3 = f32[1,128,64]{2,1,0:T(8,128)S(1)} all-reduce(f32[1,128,64]{2,1,0:T(8,128)S(1)} %broadcast_select_fusion), channel_id=7, replica_groups=mesh['expert'=64,'hidden'=16] {'expert'}, use_global_device_ids=true, to_apply=%region_8.9.clone | all-reduce | flops 8192 | bytes 65536
  508.0 2.6 convolution_bitcast_fusion
  510.5 0.0 all-reduce.6.cloned.1.call-update
  510.6 0.2 select_reduce_fusion
  510.7 0.1 multiply_reduce_fusion.1
  510.8 1.4 convolution_bitcast_fusion.2
  512.2 1.4 convolution_bitcast_fusion.1
  513.5 0.6 divide_multiply_fusion
  514.2 1.3 convolution_bitcast_fusion.3
  515.5 170.0 %all-reduce.6.cloned.1.call-done = f32[1,128,2048]{2,1,0:T(8,128)} async-done(((f32[1,128,2048]{2,1,0:T(8,128)}), f32[1,128,2048]{2,1,0:T(8,128)}) %all-reduce.6.cloned.1.call-update) | async-done | bytes 1048592
  685.5 1.5 constant_dynamic-slice_fusion
  (19 shorter events, 0.1 us)
Async XLA Ops:
  7.2 185.0 %copy-start = (bf16[1,2048,96]{1,2,0:T(8,128)(2,1)S(1)}, bf16[1,2048,96]{1,2,0:T(8,128)(2,1)}, u32[]{:S(2)}) copy-start(bf16[1,2048,96]{1,2,0:T(8,128)(2,1)} %param.11) | copy-start | bytes 1179652
  7.2 103.3 %copy-start.4 = (bf16[1,2,2048]{2,1,0:T(2,128)(2,1)S(1)}, bf16[1,2,2048]{2,1,0:T(2,128)(2,1)}, u32[]{:S(2)}) copy-start(bf16[1,2,2048]{2,1,0:T(2,128)(2,1)} %param.8) | copy-start | bytes 24580
  7.2 185.0 %all-gather.8.cloned.1.call-start = ((), (), s32[]{:S(2)}) async-start(), calls=%async_computation.2 | async-start | bytes 2228224 | tf_op jit(solution)/shard_map/all_gather | solution.py:91
  110.4 98.1 %all-gather.6.cloned.1.call-start = ((), (), s32[]{:S(2)}) async-start(), calls=%async_computation.1 | async-start | bytes 2228224 | tf_op jit(solution)/shard_map/all_gather | solution.py:92
  110.5 84.3 %copy-start.3 = (bf16[1,2048,96]{1,2,0:T(8,128)(2,1)S(1)}, bf16[1,2048,96]{1,2,0:T(8,128)(2,1)}, u32[]{:S(2)}) copy-start(bf16[1,2048,96]{1,2,0:T(8,128)(2,1)} %param.12) | copy-start | bytes 1179652
  161.3 346.6 %reduce-scatter.4.cloned.1.call-start = ((), (), s32[]{:S(2)}) async-start(), calls=%async_computation.3 | async-start | bytes 4456448 | tf_op jit(solution)/shard_map/reduce_scatter | solution.py:100
  192.2 2.6 copy-start.1
  214.3 296.2 %copy-start.5 = (s32[1,2,8]{2,1,0:T(2,128)S(1)}, s32[1,2,8]{2,1,0:T(2,128)}, u32[]{:S(2)}) copy-start(s32[1,2,8]{2,1,0:T(2,128)} %param.9) | copy-start | bytes 196
  214.4 471.2 %all-reduce.6.cloned.1.call-start = ((), (), s32[]{:S(2)}) async-start(), calls=%async_computation.4 | async-start | bytes 2097152
  512.2 1.4 copy-start.6
  512.2 2.0 copy-start.2
Sparse Core Ops, SparseCore 0:
  110.5 47.8 all-gather.7
  161.7 46.7 all-gather.5
  214.5 67.6 reduce-scatter.3
  510.7 174.8 all-reduce.5
where the time goes:
time: 695 us; the launch traced here: 694 us
  blocking collectives  467 us (67%)
  waiting for transfers between devices  183 us (26%)
  matrix products  18.2 us (3%)
  between operations  15.9 us (2%)
    unnamed x3, blocking collectives  319 us
    unnamed x5, waiting for transfers between devices  170 us
    all_gather x1, blocking collectives, on_device(): lax.all_gather(gate_table[None], 'expert', axis=1, tiled=True)  51.4 us
    all_gather x1, blocking collectives, on_device(): lax.all_gather(grad_out, 'expert', axis=1, tiled=True)  49.7 us
    all_gather x1, blocking collectives, on_device(): lax.all_gather(tokens, 'expert', axis=1, tiled=True)  47.1 us
  transfers between devices with their start and end apart: 4, of which 2 were waited for; matrix products, arithmetic and copies ran while one was open for 2% of the time, Pallas kernels for 0%

commit v1 on v0

v1 whole, which is shorter than its diff:
```python
import functools
import math

import jax
import jax.numpy as jnp
from jax import lax
from jax.experimental import pallas as pl
from jax.experimental.pallas import tpu as pltpu
from jax.sharding import PartitionSpec as P

MESH = pl.DeviceIdType.MESH
CAP = 32
LANES = 128
F32 = jnp.float32
BF16 = jnp.bfloat16


def split(value):
    lane = lax.broadcasted_iota(jnp.int32, value.shape, value.ndim - 1)
    high = value.astype(BF16).astype(F32)
    return jnp.where(lane < LANES // 2, high, value - high).astype(BF16)


def join(parts):
    wide = parts.astype(F32)
    return wide + pltpu.roll(wide, LANES // 2, 1)


def kernel(
    nx, ny, nz,
    xin, gin, wgu, wd,
    out_in, out_gate_rows, out_gate, out_up, out_down,
    a1, b1, flat_a, flat_b, a2, b2, xall, gall, dcat, scaled_t, rfull, rhalf, sib,
    ring_send_lo, ring_recv_lo, ring_send_hi, ring_recv_hi,
    c1, c1r, e1, e1r, c2, c2r, e2, e2r,
    s1a, r1a, s1b, r1b, s2a, r2a, s2b, r2b,
    sxr, rxr, sxs, rxs, sgr, rgr, sgs, rgs,
    ss, rs, slo, rlo, shi, rhi,
    s3a, r3a, s3b, r3b, s4a, r4a, s4b, r4b,
):
    mine = lax.axis_index("expert")
    hid = lax.axis_index("hidden")
    mx, my = mine // ny, mine % ny
    mz, core = hid // 2, hid % 2
    dim = wd.shape[1]
    units = wd.shape[0]
    half = dim // 2
    tokens = 2 * nx * ny
    padded = dim + LANES

    def at_x(x):
        return {"expert": x * ny + my, "hidden": hid}

    def at_y(y):
        return {"expert": mx * ny + y, "hidden": hid}

    def at_z(z):
        return {"expert": mine, "hidden": 2 * z + core}

    sibling = {"expert": mine, "hidden": 2 * mz + 1 - core}
    up_z, down_z = (mz + 1) % nz, (mz + nz - 1) % nz
    pending = []

    def send(src, dst, send_sem, recv_sem, device):
        copy = pltpu.make_async_remote_copy(
            src_ref=src, dst_ref=dst, send_sem=send_sem, recv_sem=recv_sem,
            device_id=device, device_id_type=MESH,
        )
        copy.start()
        pending.append(copy)
        return copy

    barrier = pltpu.get_barrier_semaphore()
    greet = [at_x((mx + d) % nx) for d in range(1, nx)]
    greet += [at_y((my + d) % ny) for d in range(1, ny)]
    greet += [at_z(up_z), at_z(down_z), sibling]
    for device in greet:
        pl.semaphore_signal(barrier, inc=1, device_id=device, device_id_type=MESH)
    pl.semaphore_wait(barrier, len(greet))

    a_sends = [
        send(xin, a1.at[mx], s1a.at[d], r1a.at[d], at_x((mx + d) % nx)) for d in range(1, nx)
    ]
    b_sends = [
        send(gin, b1.at[my], s1b.at[d], r1b.at[d], at_y((my + d) % ny)) for d in range(1, ny)
    ]
    a1[mx] = xin[...]
    b1[my] = gin[...]
    for copy in a_sends:
        copy.wait_recv()
    for k in range(nx):
        flat_a[2 * k : 2 * k + 2, :] = a1[k].astype(F32)
    a2[my] = flat_a[...].astype(BF16)
    a_sends = [
        send(a2.at[my], a2.at[my], s2a.at[d], r2a.at[d], at_y((my + d) % ny)) for d in range(1, ny)
    ]
    for copy in b_sends:
        copy.wait_recv()
    for k in range(ny):
        flat_b[2 * k : 2 * k + 2, :] = b1[k].astype(F32)
    b2[mx] = flat_b[...].astype(BF16)
    b_sends = [
        send(b2.at[mx], b2.at[mx], s2b.at[d], r2b.at[d], at_x((mx + d) % nx)) for d in range(1, nx)
    ]

    lane = lax.broadcasted_iota(jnp.int32, (8, LANES), 1)
    own_lane = jnp.where(lane == mine, 1.0, 0.0).astype(BF16)

    def order_b(t):
        xx, yy, jj = t // (2 * ny), (t // 2) % ny, t % 2
        return (yy * nx + xx) * 2 + jj

    def placing_of(table, order):
        gate = lax.dot_general(own_lane, table, (((1,), (1,)), ((), ())), preferred_element_type=F32)
        picked = jnp.where(gate > 0.0, 1.0, 0.0)
        before = order(lax.broadcasted_iota(jnp.int32, (tokens, tokens), 0))
        after = order(lax.broadcasted_iota(jnp.int32, (tokens, tokens), 1))
        upto = jnp.where(before <= after, 1.0, 0.0).astype(BF16)
        rank = jnp.dot(picked.astype(BF16), upto, preferred_element_type=F32) - 1.0
        rank = jnp.where(picked > 0.0, rank, -1.0)
        slot = lax.broadcasted_iota(jnp.int32, (CAP, tokens), 0).astype(F32)
        return jnp.where(rank[0:1, :] == slot, 1.0, 0.0)

    for copy in a_sends:
        copy.wait_recv()
    all_a = a2[...].reshape(tokens, padded)
    place_a = placing_of(all_a[:, dim:], lambda t: t)
    xall[hid] = jnp.dot(place_a.astype(BF16), all_a, preferred_element_type=F32).astype(BF16)

    def ring_start(buf, sems, cross, up_hops):
        own = buf.at[hid]
        first = [
            send(own, own, sems[0].at[0, 0], sems[1].at[0, 0], at_z(up_z)),
            send(own, own, sems[0].at[1, 0], sems[1].at[1, 0], at_z(down_z)),
        ]
        over = [send(own, own, cross[0].at[0], cross[1].at[0], sibling)]
        return first, over

    def ring_step(buf, sems, cross, hops, state, step):
        waits, over = state
        for side, sign in ((0, 1), (1, -1)):
            if step >= hops[side]:
                continue
            waits[side].wait_recv()
            block = buf.at[2 * ((mz - sign * (step + 1) + nz) % nz) + core]
            if step + 1 < hops[side]:
                waits[side] = send(
                    block, block, sems[0].at[side, step + 1], sems[1].at[side, step + 1],
                    at_z(up_z if side == 0 else down_z),
                )
            number = 1 + 2 * step + side
            over.append(send(block, block, cross[0].at[number], cross[1].at[number], sibling))

    long, short = nz // 2, nz // 2 - 1
    x_state = ring_start(xall, (sxr, rxr), (sxs, rxs), long)
    for copy in b_sends:
        copy.wait_recv()
    all_b = b2[...].reshape(tokens, padded)
    place_b = placing_of(all_b[:, dim:], order_b)
    gall[hid] = jnp.dot(
        place_b.astype(BF16), all_b[:, :dim], preferred_element_type=F32
    ).astype(BF16)
    g_state = ring_start(gall, (sgr, rgr), (sgs, rgs), short)
    for step in range(long):
        ring_step(xall, (sxr, rxr), (sxs, rxs), (long, short), x_state, step)
        ring_step(gall, (sgr, rgr), (sgs, rgs), (short, long), g_state, step)
    for copy in x_state[1] + g_state[1]:
        copy.wait_recv()

    per = LANES // CAP

    def group(g, _):
        at = pl.ds(g * per, per)
        cols = pl.ds(pl.multiple_of(g * LANES, LANES), LANES)
        xs = xall[at].reshape(LANES, padded)
        gs = gall[at].reshape(LANES, dim)
        both = lax.dot_general(wgu[...], xs[:, :dim], (((1,), (1,)), ((), ())), preferred_element_type=F32)
        pre_gate, pre_up = both[:units], both[units:]
        back = lax.dot_general(wd[...], gs, (((1,), (1,)), ((), ())), preferred_element_type=F32)
        weight = lax.dot_general(
            own_lane, xs[:, dim:], (((1,), (1,)), ((), ())), preferred_element_type=F32
        )[0:1, :]
        sigmoid = 1.0 / (1.0 + jnp.exp(-pre_gate))
        silu = pre_gate * sigmoid
        active = silu * pre_up
        total = jnp.sum(active * back, axis=0, keepdims=True)
        total = jnp.transpose(jnp.broadcast_to(total, (LANES, LANES)))
        scaled_t[:, cols] = (weight * active).astype(BF16)
        weighted = weight * back
        d_gate = (weighted * pre_up * sigmoid * (1.0 + pre_gate * (1.0 - sigmoid))).astype(BF16)
        d_up = (weighted * silu).astype(BF16)
        dcat[:units, cols] = d_gate
        dcat[units:, cols] = d_up
        rows = lax.dot_general(
            dcat[:, cols], wgu[...], (((0,), (0,)), ((), ())), preferred_element_type=F32
        ).reshape(per, CAP, dim)
        rfull[at, :, :dim] = rows
        rhalf[at, :, :dim] = rows.astype(BF16)
        rfull[at, :, dim:] = total.reshape(per, CAP, LANES)
        rhalf[at, :, dim:] = split(total).reshape(per, CAP, LANES)
        return 0

    lax.fori_loop(0, 2 * nz // per, group, 0)

    crossing = []
    for d in range(nz):
        z = (mz + nz // 2 + d) % nz
        crossing.append(
            send(rhalf.at[2 * z + 1 - core], sib.at[z], ss.at[d], rs.at[d], sibling)
        )

    tile = min(512, dim)

    def weights(n, _):
        cols = pl.ds(pl.multiple_of(n * tile, tile), tile)
        flat = 2 * nz * CAP
        grads = jnp.dot(dcat[...], xall[:, :, cols].reshape(flat, tile), preferred_element_type=F32)
        out_gate[:, cols] = grads[:units]
        out_up[:, cols] = grads[units:]
        out_down[:, cols] = jnp.dot(
            scaled_t[...], gall[:, :, cols].reshape(flat, tile), preferred_element_type=F32
        )
        return 0

    lax.fori_loop(0, dim // tile, weights, 0)
    for copy in crossing:
        copy.wait_recv()

    def low_part(z):
        return rfull[2 * z + core, :, :half] + sib[z, :, :half].astype(F32)

    def high_part(z):
        return rfull[2 * z + core, :, half:dim] + sib[z, :, half:dim].astype(F32)

    def gate_part(z):
        return rfull[2 * z + core, :, dim:] + join(sib[z, :, dim:])

    last = {}
    for step in range(long):
        for side, sign in ((0, 1), (1, -1)):
            to = at_z(up_z if side == 0 else down_z)
            hops = long if side == 0 else short
            if step < hops:
                if step:
                    last["lo", side].wait_recv()
                z = (mz + sign * (hops - step) + nz) % nz
                value = low_part(z)
                if step:
                    value = value + ring_recv_lo[side, step - 1].astype(F32)
                ring_send_lo[side, step] = value.astype(BF16)
                last["lo", side] = send(
                    ring_send_lo.at[side, step], ring_recv_lo.at[side, step],
                    slo.at[side, step], rlo.at[side, step], to,
                )
            hops = short if side == 0 else long
            if step < hops:
                if step:
                    last["hi", side].wait_recv()
                z = (mz + sign * (hops - step) + nz) % nz
                value, gate_value = high_part(z), gate_part(z)
                if step:
                    value = value + ring_recv_hi[side, step - 1, :, :half].astype(F32)
                    gate_value = gate_value + join(ring_recv_hi[side, step - 1, :, half:])
                ring_send_hi[side, step, :, :half] = value.astype(BF16)
                ring_send_hi[side, step, :, half:] = split(gate_value)
                last["hi", side] = send(
                    ring_send_hi.at[side, step], ring_recv_hi.at[side, step],
                    shi.at[side, step], rhi.at[side, step], to,
                )

    def back_to_tokens(place, rows):
        return lax.dot_general(
            place.astype(BF16), rows, (((0,), (0,)), ((), ())), preferred_element_type=F32
        ).astype(BF16)

    low = low_part(mz)
    for side, hops in ((0, long), (1, short)):
        last["lo", side].wait_recv()
        low = low + ring_recv_lo[side, hops - 1].astype(F32)
    c1[...] = back_to_tokens(place_a, low.astype(BF16)).reshape(ny, 2 * nx, half)
    c_sends = []
    for d in range(1, ny):
        y = (my + d) % ny
        c_sends.append(send(c1.at[y], c1r.at[my], s3a.at[d], r3a.at[d], at_y(y)))
    c1r[my] = c1[my]

    high, gate_row = high_part(mz), gate_part(mz)
    for side, hops in ((0, short), (1, long)):
        last["hi", side].wait_recv()
        high = high + ring_recv_hi[side, hops - 1, :, :half].astype(F32)
        gate_row = gate_row + join(ring_recv_hi[side, hops - 1, :, half:])
    lanes = lax.broadcasted_iota(jnp.int32, (CAP, LANES), 1)
    gate_row = jnp.where(lanes % (LANES // 2) == mine, split(gate_row).astype(F32), 0.0).astype(BF16)
    e1[:, :, :half] = back_to_tokens(place_b, high.astype(BF16)).reshape(nx, 2 * ny, half)
    e1[:, :, half:] = back_to_tokens(place_b, gate_row).reshape(nx, 2 * ny, LANES)
    e_sends = []
    for d in range(1, nx):
        x = (mx + d) % nx
        e_sends.append(send(e1.at[x], e1r.at[mx], s3b.at[d], r3b.at[d], at_x(x)))
    e1r[mx] = e1[mx]

    def total_of(buf, count):
        value = buf[0].astype(F32)
        for k in range(1, count):
            value = value + buf[k].astype(F32)
        return value

    for copy in c_sends:
        copy.wait_recv()
    flat_a[:, :half] = total_of(c1r, ny)
    for k in range(nx):
        c2[k] = flat_a[2 * k : 2 * k + 2, :half]
    c_sends = []
    for d in range(1, nx):
        x = (mx + d) % nx
        c_sends.append(send(c2.at[x], c2r.at[mx], s4a.at[d], r4a.at[d], at_x(x)))
    c2r[mx] = c2[mx]

    for copy in e_sends:
        copy.wait_recv()
    flat_b[:, : half + LANES] = total_of(e1r, nx)
    for k in range(ny):
        e2[k] = flat_b[2 * k : 2 * k + 2, : half + LANES]
    e_sends = []
    for d in range(1, ny):
        y = (my + d) % ny
        e_sends.append(send(e2.at[y], e2r.at[my], s4b.at[d], r4b.at[d], at_y(y)))
    e2r[my] = e2[my]

    for copy in c_sends:
        copy.wait_recv()
    out_in[:, :half] = total_of(c2r, nx)
    for copy in e_sends:
        copy.wait_recv()
    final = total_of(e2r, ny)
    out_in[:, half:] = final[:, :half]
    out_gate_rows[...] = final[:, half:]
    for copy in pending:
        copy.wait_send()


def on_device(nx, ny, nz, tokens, grad_out, expert_ids, router_logits, w_gate, w_up, w_down):
    peers = nx * ny
    dim, units = w_gate.shape[1], w_gate.shape[2]
    padded, half = dim + LANES, dim // 2
    long = nz // 2
    raised = jnp.exp(router_logits[0])
    gate_probs = raised / jnp.sum(raised, axis=-1, keepdims=True)
    gate_rows = gate_probs.astype(BF16)
    chosen = expert_ids[0][:, :, None] == jnp.arange(LANES, dtype=jnp.int32)[None, None, :]
    table = jnp.sum(jnp.where(chosen, gate_rows.astype(F32)[:, :, None], 0.0), axis=1).astype(BF16)
    xin = jnp.concatenate([tokens[0], table], axis=1)
    gin = jnp.concatenate([grad_out[0], table], axis=1)
    wgu = jnp.concatenate([jnp.swapaxes(w_gate[0], 0, 1), jnp.swapaxes(w_up[0], 0, 1)], axis=0)
    vmem, dma = pltpu.VMEM, pltpu.SemaphoreType.DMA
    wide = half + LANES
    scratch = [
        vmem((nx, 2, padded), BF16), vmem((ny, 2, padded), BF16),
        vmem((2 * nx, padded), F32), vmem((2 * ny, padded), F32),
        vmem((ny, 2 * nx, padded), BF16), vmem((nx, 2 * ny, padded), BF16),
        vmem((2 * nz, CAP, padded), BF16), vmem((2 * nz, CAP, dim), BF16),
        vmem((2 * units, 2 * nz * CAP), BF16), vmem((units, 2 * nz * CAP), BF16),
        vmem((2 * nz, CAP, padded), F32), vmem((2 * nz, CAP, padded), BF16),
        vmem((nz, CAP, padded), BF16),
        vmem((2, long, CAP, half), BF16), vmem((2, long, CAP, half), BF16),
        vmem((2, long, CAP, wide), BF16), vmem((2, long, CAP, wide), BF16),
        vmem((ny, 2 * nx, half), BF16), vmem((ny, 2 * nx, half), BF16),
        vmem((nx, 2 * ny, wide), BF16), vmem((nx, 2 * ny, wide), BF16),
        vmem((nx, 2, half), F32), vmem((nx, 2, half), F32),
        vmem((ny, 2, wide), F32), vmem((ny, 2, wide), F32),
    ]
    for count in (nx, nx, ny, ny, ny, ny, nx, nx):
        scratch.append(dma((count,)))
    for _ in range(2):
        scratch += [dma((2, long)), dma((2, long)), dma((2 * long + 1,)), dma((2 * long + 1,))]
    scratch += [dma((nz,)), dma((nz,)), dma((2, long)), dma((2, long)), dma((2, long)), dma((2, long))]
    for count in (ny, ny, nx, nx, nx, nx, ny, ny):
        scratch.append(dma((count,)))
    spec = pl.BlockSpec(memory_space=pltpu.VMEM)
    rows, gate_dense, sum_gate, sum_up, sum_down = pl.pallas_call(
        functools.partial(kernel, nx, ny, nz),
        out_shape=[
            jax.ShapeDtypeStruct((2, dim), F32),
            jax.ShapeDtypeStruct((2, LANES), F32),
            jax.ShapeDtypeStruct((units, dim), F32),
            jax.ShapeDtypeStruct((units, dim), F32),
            jax.ShapeDtypeStruct((units, dim), F32),
        ],
        in_specs=[spec] * 4,
        out_specs=[spec] * 5,
        scratch_shapes=scratch,
        compiler_params=pltpu.CompilerParams(
            collective_id=0, has_side_effects=True, vmem_limit_bytes=56 * 1024 * 1024
        ),
    )(xin, gin, wgu, w_down[0])
    per_expert = gate_dense[:, : LANES // 2] + gate_dense[:, LANES // 2 :]
    gate_grad = jnp.sum(
        jnp.where(chosen[:, :, : LANES // 2], per_expert[:, None, :], 0.0), axis=-1
    )
    grad_logits = gate_probs * (gate_grad - jnp.sum(gate_probs * gate_grad, axis=-1, keepdims=True))
    return (
        rows[None],
        grad_logits[None],
        jnp.swapaxes(sum_gate, 0, 1)[None],
        jnp.swapaxes(sum_up, 0, 1)[None],
        sum_down[None],
    )


def solution(mesh):
    side = math.isqrt(mesh.shape["expert"])
    nz = mesh.shape["hidden"] // 2
    token_spec, wide, tall = P("hidden", "expert", None), P("expert", None, "hidden"), P("expert", "hidden", None)
    return jax.shard_map(
        functools.partial(on_device, side, side, nz),
        mesh=mesh,
        in_specs=(token_spec,) * 4 + (wide, wide, tall),
        out_specs=(token_spec, token_spec, wide, wide, tall),
        check_vma=False,
    )
```

time: 695 us -> 122 us (0.18)
  blocking collectives: 467 us -> 0 us
  waiting for transfers between devices: 183 us -> 0 us
  Pallas kernels: 0 us -> 107 us
  matrix products: 18.2 us -> 0 us
  between operations: 15.9 us -> 0.65 us
    unnamed x3 -> x0, blocking collectives: 319 us -> none
    unnamed x5 -> x0, waiting for transfers between devices: 170 us -> none
    all_gather x3 -> x0, blocking collectives: 148 us -> none  [the longest x1 51.4 us: on_device(): lax.all_gather(gate_table[None], 'expert', axis=1, tiled=True)]
    pallas_call x0 -> x1, Pallas kernels: none -> 107 us  [on_device(): pl.pallas_call(functools.partial(kernel, nx, ny, nz), out_shape=[jax.Shap...]
    dot_general x13 -> x0, matrix products: 18.2 us -> none  [the longest x1 2.66 us: project_back(): lax.dot_general(d_up_pre, up_weight, (((1,), (1,)), ((), ())), preferred_...]
    all_gather x2 -> x0, waiting for transfers between devices: 12.9 us -> none  [the longest x1 12.9 us: on_device(): lax.all_gather(grad_rows, 'hidden', axis=0, tiled=True)]
  transfers between devices with their start and end apart: 4 -> 0, of which waited for: 2 -> 0; matrix products, arithmetic and copies ran while one was open for 2% -> 0% of each run, Pallas kernels for 0% -> 0%
where the time goes in v1:
time: 122 us; the launch traced here: 121 us
  Pallas kernels  107 us (88%)
  other arithmetic  7.46 us (6%)
  local copies, waits for them, and re-layouts  5.76 us (5%)
    pallas_call x1, Pallas kernels, on_device(): pl.pallas_call(functools.partial(kernel, nx, ny, nz), out_shape=[jax.Shap...  107 us
    unnamed x12, local copies, waits for them, and re-layouts  5.76 us

profile of v1, /device:TPU:14, one launch (start us, length us, event | category | flops | bytes accessed | tf_op | source)
XLA Modules:
  0.0 121.1 jit_solution(8545611871242288583)
XLA Ops:
  0.6 0.8 exponential_reduce_fusion
  1.4 0.8 convert_convert_fusion
  2.2 0.8 select_reduce_fusion.1
  3.0 1.3 %pad_maximum_fusion.2 = (bf16[2,2176]{1,0:T(2,128)(2,1)}, bf16[2,2176]{1,0:T(2,128)(2,1)}) fusion(bf16[2,2048]{1,0:T(2,128)(2,1)} %bitcast.32, bf16[2,128]{1,0:T(2,128)(2,1)S(1)} %select_reduce_fusion.1, bf16[2,2048]{1,0:T(2,128)(2,1)} %bitcast.33), kind=kLoop, calls=%fused_computation.2 | loop fusion | flops 30464 | bytes 34304 | tf_op jit(solution)/shard_map/concatenate | solution.py:353
  4.3 2.1 %pad_maximum_fusion.wgu = bf16[192,2048]{1,0:T(8,128)(2,1)} fusion(bf16[96,2048]{1,0:T(8,128)(2,1)} %bitcast.28, bf16[96,2048]{1,0:T(8,128)(2,1)} %bitcast.29), kind=kLoop, calls=%fused_computation | loop fusion | flops 1572864 | bytes 1572864 | tf_op jit(solution)/shard_map/concatenate | solution.py:354
  6.4 0.0 copy-start.2
  6.4 0.0 copy-start.3
  6.4 107.3 %shard_map.110 = (f32[2,2048]{1,0:T(2,128)}, f32[2,128]{1,0:T(2,128)}, f32[96,2048]{1,0:T(8,128)}, f32[96,2048]{1,0:T(8,128)}, f32[96,2048]{1,0:T(8,128)}) custom-call(bf16[2,2176]{1,0:T(2,128)(2,1)} %get-tuple-element.18.xin, bf16[2,2176]{1,0:T(2,128)(2,1)} %get-tuple-element.17.gin, bf16[192,2048]{1,0:T(8,128)(2,1)} %pad_maximum_fusion.wgu, ...), custom_call_target="tpu_custom_call" | custom-call | tf_op jit(solution)/shard_map/pallas_call | solution.py:380
  113.6 0.8 slice_add_fusion
  114.4 0.0 copy-done.2
  114.4 0.1 iota_compare_fusion
  114.5 0.1 select_reduce_fusion
  114.6 0.1 multiply_reduce_fusion
  114.7 0.0 copy-done.3
  114.7 0.6 divide_multiply_fusion
  115.4 1.3 %copy.16 = f32[1,2,2048]{2,1,0:T(2,128)} copy(f32[1,2,2048]{2,1,0:T(2,128)} %bitcast.31) | data formatting | bytes 32768
  116.7 0.0 copy-start.1
  116.7 2.1 %copy.17 = f32[1,2048,96]{1,2,0:T(8,128)} copy(f32[1,2048,96]{1,2,0:T(8,128)} %bitcast.27) | data formatting | bytes 1572864
  118.8 0.0 copy-done.1
  118.8 0.0 copy-start
  118.8 0.9 copy.18
  119.7 0.5 copy-done
  120.3 0.9 copy.19
Async XLA Ops:
  6.4 108.1 %copy-start.2 = (s32[1,2,8]{2,1,0:T(2,128)S(1)}, s32[1,2,8]{2,1,0:T(2,128)}, u32[]{:S(2)}) copy-start(s32[1,2,8]{2,1,0:T(2,128)} %param.9) | copy-start | bytes 196
  6.4 108.4 %copy-start.3 = (f32[1,2,8]{2,1,0:T(2,128)S(1)}, f32[1,2,8]{2,1,0:T(2,128)}, u32[]{:S(2)}) copy-start(f32[1,2,8]{2,1,0:T(2,128)} %param.10) | copy-start | bytes 196
  116.7 2.1 %copy-start.1 = (f32[96,2048]{1,0:T(8,128)S(1)}, f32[96,2048]{1,0:T(8,128)}, u32[]{:S(2)}) copy-start(f32[96,2048]{1,0:T(8,128)} %get-tuple-element.13) | copy-start | bytes 2359300
  118.8 1.4 %copy-start = (f32[96,2048]{1,0:T(8,128)S(1)}, f32[96,2048]{1,0:T(8,128)}, u32[]{:S(2)}) copy-start(f32[96,2048]{1,0:T(8,128)} %get-tuple-element.14) | copy-start | bytes 2359300

commit v2 on v0

v2 whole, which is shorter than its diff:
```python
import functools
import math

import jax
import jax.numpy as jnp
from jax import lax
from jax.experimental import pallas as pl
from jax.experimental.pallas import tpu as pltpu
from jax.sharding import PartitionSpec as P

MESH = pl.DeviceIdType.MESH
CAP = 32
LANES = 128
F32 = jnp.float32
BF16 = jnp.bfloat16
TRANSPOSED_RIGHT = (((1,), (1,)), ((), ()))
TRANSPOSED_LEFT = (((0,), (0,)), ((), ()))


def split(value):
    lane = lax.broadcasted_iota(jnp.int32, value.shape, value.ndim - 1)
    high = value.astype(BF16).astype(F32)
    return jnp.where(lane < LANES // 2, high, value - high).astype(BF16)


def join(parts):
    wide = parts.astype(F32)
    return wide + pltpu.roll(wide, LANES // 2, 1)


def sections_of(dim):
    half, quarter = dim // 2, dim // 4
    return [
        (True, 0, quarter, False),
        (False, half, quarter, True),
        (True, quarter, quarter, False),
        (False, half + quarter, quarter, False),
    ]


def scratch_of(nx, ny, nz, dim, units):
    vmem, dma = pltpu.VMEM, pltpu.SemaphoreType.DMA
    half, padded, long = dim // 2, dim + LANES, nz // 2
    wide = half + LANES
    flat = 2 * nz * CAP
    shapes = {
        "xa": vmem((2, wide), BF16), "xb": vmem((2, wide), BF16),
        "xa1": vmem((nx, 2, wide), BF16), "xb1": vmem((ny, 2, wide), BF16),
        "ga1": vmem((nx, 2, half), BF16), "gb1": vmem((ny, 2, half), BF16),
        "flat_a": vmem((2 * nx, wide), F32), "flat_b": vmem((2 * ny, wide), F32),
        "xa2": vmem((ny, 2 * nx, wide), BF16), "xb2": vmem((nx, 2 * ny, wide), BF16),
        "ga2": vmem((ny, 2 * nx, half), BF16), "gb2": vmem((nx, 2 * ny, half), BF16),
        "xlo": vmem((2 * nz, CAP, half), BF16), "xhi": vmem((2 * nz, CAP, wide), BF16),
        "glo": vmem((2 * nz, CAP, half), BF16), "ghi": vmem((2 * nz, CAP, half), BF16),
        "wgu": vmem((2 * units, dim), BF16), "wd": vmem((units, dim), BF16),
        "pre": vmem((2 * units, flat), F32), "weight": vmem((8, flat), F32),
        "dcat": vmem((2 * units, flat), BF16), "scaled": vmem((units, flat), BF16),
        "rfull": vmem((2 * nz, CAP, padded), F32), "rhalf": vmem((2 * nz, CAP, padded), BF16),
        "sib": vmem((nz, CAP, padded), BF16),
        "sums": vmem((2 * units, dim), F32), "sums_down": vmem((units, dim), F32),
        "ssem": dma((256,)), "rsem": dma((256,)), "lsem": dma((8,)),
    }
    for n, (first_y, _, width, gate) in enumerate(sections_of(dim)):
        size = width + (LANES if gate else 0)
        one, two = (ny, nx) if first_y else (nx, ny)
        shapes[f"put{n}"] = vmem((2, long, CAP, size), BF16)
        shapes[f"got{n}"] = vmem((2, long, CAP, size), BF16)
        shapes[f"c{n}"] = vmem((one, 2 * two, size), BF16)
        shapes[f"cr{n}"] = vmem((one, 2 * two, size), BF16)
        shapes[f"e{n}"] = vmem((two, 2, size), F32)
        shapes[f"er{n}"] = vmem((two, 2, size), F32)
        shapes[f"flat{n}"] = vmem((2 * two, size), F32)
    return shapes


def kernel(
    nx, ny, nz, names,
    tok, grd, ids, logits, wg, wu, wdn,
    out_in, out_logits, out_gate, out_up, out_down, *scratch,
):
    s = dict(zip(names, scratch))
    mine = lax.axis_index("expert")
    hid = lax.axis_index("hidden")
    mx, my = mine // ny, mine % ny
    mz, core = hid // 2, hid % 2
    units, dim = wdn.shape
    top = ids.shape[1]
    half = dim // 2
    tokens = 2 * nx * ny
    long, short = nz // 2, nz // 2 - 1

    def at_x(x):
        return {"expert": x * ny + my, "hidden": hid}

    def at_y(y):
        return {"expert": mx * ny + y, "hidden": hid}

    def at_z(z):
        return {"expert": mine, "hidden": 2 * z + core}

    sibling = {"expert": mine, "hidden": 2 * mz + 1 - core}
    up_z, down_z = (mz + 1) % nz, (mz + nz - 1) % nz
    pending = []

    def send(src, dst, device):
        number = len(pending)
        copy = pltpu.make_async_remote_copy(
            src_ref=src, dst_ref=dst, send_sem=s["ssem"].at[number], recv_sem=s["rsem"].at[number],
            device_id=device, device_id_type=MESH,
        )
        copy.start()
        pending.append(copy)
        return copy

    def arrive(copies):
        for copy in copies:
            copy.wait_recv()

    barrier = pltpu.get_barrier_semaphore()
    greet = [at_x((mx + d) % nx) for d in range(1, nx)]
    greet += [at_y((my + d) % ny) for d in range(1, ny)]
    greet += [at_z(up_z), at_z(down_z), sibling]
    for device in greet:
        pl.semaphore_signal(barrier, inc=1, device_id=device, device_id_type=MESH)

    loads = [
        pltpu.make_async_copy(wg, s["wgu"].at[pl.ds(0, units)], s["lsem"].at[0]),
        pltpu.make_async_copy(wu, s["wgu"].at[pl.ds(units, units)], s["lsem"].at[1]),
        pltpu.make_async_copy(wdn, s["wd"], s["lsem"].at[2]),
    ]
    for load in loads:
        load.start()

    raised = jnp.exp(logits[...])
    probs = raised / jnp.sum(raised, axis=-1, keepdims=True)
    lane_of = lax.broadcasted_iota(jnp.int32, (2, LANES), 1)
    hits = [lane_of == ids[:, k : k + 1] for k in range(top)]
    spread = jnp.zeros((2, LANES), F32)
    for k in range(top):
        spread = spread + jnp.where(hits[k], probs[:, k : k + 1], 0.0)
    table = spread.astype(BF16)
    s["xa"][:, :half] = tok[:, :half]
    s["xb"][:, :half] = tok[:, half:]
    s["xa"][:, half:] = table
    s["xb"][:, half:] = table
    pl.semaphore_wait(barrier, len(greet))

    def spread_x(src, dst):
        return [send(src, dst.at[mx], at_x((mx + d) % nx)) for d in range(1, nx)]

    def spread_y(src, dst):
        return [send(src, dst.at[my], at_y((my + d) % ny)) for d in range(1, ny)]

    xa = spread_x(s["xa"], s["xa1"])
    xb = spread_y(s["xb"], s["xb1"])
    s["xa1"][mx] = s["xa"][...]
    s["xb1"][my] = s["xb"][...]
    ga = spread_x(grd.at[:, pl.ds(0, half)], s["ga1"])
    gb = spread_y(grd.at[:, pl.ds(half, half)], s["gb1"])
    s["ga1"][mx] = grd[:, :half]
    s["gb1"][my] = grd[:, half:]

    def flatten(blocks, wide):
        count, _, width = blocks.shape
        for k in range(count):
            wide[2 * k : 2 * k + 2, :width] = blocks[k].astype(F32)
        return wide[:, :width].astype(BF16)

    arrive(xa)
    s["xa2"][my] = flatten(s["xa1"], s["flat_a"])
    xa = spread_y(s["xa2"].at[my], s["xa2"])
    arrive(xb)
    s["xb2"][mx] = flatten(s["xb1"], s["flat_b"])
    xb = spread_x(s["xb2"].at[mx], s["xb2"])
    arrive(ga)
    s["ga2"][my] = flatten(s["ga1"], s["flat_a"])
    ga = spread_y(s["ga2"].at[my], s["ga2"])
    arrive(gb)
    s["gb2"][mx] = flatten(s["gb1"], s["flat_b"])
    gb = spread_x(s["gb2"].at[mx], s["gb2"])

    own_lane = jnp.where(lax.broadcasted_iota(jnp.int32, (8, LANES), 1) == mine, 1.0, 0.0).astype(BF16)

    def order_a(t):
        return t

    def order_b(t):
        xx, yy, jj = t // (2 * ny), (t // 2) % ny, t % 2
        return (yy * nx + xx) * 2 + jj

    def placing_of(gates, order):
        gate = lax.dot_general(own_lane, gates, TRANSPOSED_RIGHT, preferred_element_type=F32)
        picked = jnp.where(gate > 0.0, 1.0, 0.0)
        before = order(lax.broadcasted_iota(jnp.int32, (tokens, tokens), 0))
        after = order(lax.broadcasted_iota(jnp.int32, (tokens, tokens), 1))
        upto = jnp.where(before <= after, 1.0, 0.0).astype(BF16)
        rank = jnp.dot(picked.astype(BF16), upto, preferred_element_type=F32) - 1.0
        rank = jnp.where(picked > 0.0, rank, -1.0)
        slot = lax.broadcasted_iota(jnp.int32, (CAP, tokens), 0).astype(F32)
        return jnp.where(rank[0:1, :] == slot, 1.0, 0.0).astype(BF16)

    def ring_start(buf, hops):
        own = buf.at[hid]
        waits = [send(own, own, at_z(up_z)), send(own, own, at_z(down_z))]
        return buf, hops, waits, [send(own, own, sibling)]

    def ring_step(ring, step):
        buf, hops, waits, over = ring
        for side, sign in ((0, 1), (1, -1)) if hops[0] >= hops[1] else ((1, -1), (0, 1)):
            if step >= hops[side]:
                continue
            waits[side].wait_recv()
            block = buf.at[2 * ((mz - sign * (step + 1) + nz) % nz) + core]
            if step + 1 < hops[side]:
                waits[side] = send(block, block, at_z(up_z if side == 0 else down_z))
            over.append(send(block, block, sibling))

    arrive(xa)
    wide_a = s["xa2"][...].reshape(tokens, half + LANES)
    place_a = placing_of(wide_a[:, half:], order_a)
    s["xlo"][hid] = jnp.dot(place_a, wide_a[:, :half], preferred_element_type=F32).astype(BF16)
    x_low = ring_start(s["xlo"], (long, short))
    arrive(xb)
    wide_b = s["xb2"][...].reshape(tokens, half + LANES)
    place_b = placing_of(wide_b[:, half:], order_b)
    s["xhi"][hid] = jnp.dot(place_b, wide_b, preferred_element_type=F32).astype(BF16)
    x_high = ring_start(s["xhi"], (short, long))
    ring_step(x_low, 0)
    ring_step(x_high, 0)
    arrive(ga)
    s["glo"][hid] = jnp.dot(
        place_a, s["ga2"][...].reshape(tokens, half), preferred_element_type=F32
    ).astype(BF16)
    g_low = ring_start(s["glo"], (long, short))
    arrive(gb)
    s["ghi"][hid] = jnp.dot(
        place_b, s["gb2"][...].reshape(tokens, half), preferred_element_type=F32
    ).astype(BF16)
    g_high = ring_start(s["ghi"], (short, long))
    for step in range(1, long):
        ring_step(x_low, step)
        ring_step(x_high, step)
        ring_step(g_low, step - 1)
        ring_step(g_high, step - 1)
    arrive(x_low[3] + x_high[3])

    def z_at(p):
        step = (p + 1) // 2
        return (mz + nz // 2 + (1 - 2 * (p % 2)) * step + nz) % nz

    def rows_at(buf, p, columns):
        return buf[pl.ds(2 * z_at(p), 2), :, columns].reshape(2 * CAP, -1)

    pair = LANES // (2 * CAP)

    def rows_of(buf, g, columns):
        return jnp.concatenate([rows_at(buf, g * pair + i, columns) for i in range(pair)], axis=0)

    for load in loads:
        load.wait()
    every, low, high = slice(None), slice(0, half), slice(half, dim)

    def forward(g, _):
        cols = pl.ds(pl.multiple_of(g * LANES, LANES), LANES)
        x_hi = rows_of(s["xhi"], g, every)
        s["pre"][:, cols] = lax.dot_general(
            s["wgu"][:, low], rows_of(s["xlo"], g, every), TRANSPOSED_RIGHT, preferred_element_type=F32
        ) + lax.dot_general(
            s["wgu"][:, high], x_hi[:, :half], TRANSPOSED_RIGHT, preferred_element_type=F32
        )
        s["weight"][:, cols] = lax.dot_general(
            own_lane, x_hi[:, half:], TRANSPOSED_RIGHT, preferred_element_type=F32
        )
        return 0

    groups = nz // pair
    lax.fori_loop(0, groups, forward, 0)
    ring_step(g_low, long - 1)
    ring_step(g_high, long - 1)
    arrive(g_low[3] + g_high[3])

    crossing = []
    for g in range(groups):
        cols = slice(g * LANES, (g + 1) * LANES)
        back = lax.dot_general(
            s["wd"][:, low], rows_of(s["glo"], g, every), TRANSPOSED_RIGHT, preferred_element_type=F32
        ) + lax.dot_general(
            s["wd"][:, high], rows_of(s["ghi"], g, every), TRANSPOSED_RIGHT, preferred_element_type=F32
        )
        pre_gate, pre_up = s["pre"][:units, cols], s["pre"][units:, cols]
        weight = s["weight"][0:1, cols]
        sigmoid = 1.0 / (1.0 + jnp.exp(-pre_gate))
        silu = pre_gate * sigmoid
        active = silu * pre_up
        total = jnp.sum(active * back, axis=0, keepdims=True)
        total = jnp.transpose(jnp.broadcast_to(total, (LANES, LANES)))
        s["scaled"][:, cols] = (weight * active).astype(BF16)
        weighted = weight * back
        s["dcat"][:units, cols] = (
            weighted * pre_up * sigmoid * (1.0 + pre_gate * (1.0 - sigmoid))
        ).astype(BF16)
        s["dcat"][units:, cols] = (weighted * silu).astype(BF16)
        rows = lax.dot_general(
            s["dcat"][:, cols], s["wgu"][...], TRANSPOSED_LEFT, preferred_element_type=F32
        )
        for i in range(pair):
            z = z_at(g * pair + i)
            part = slice(2 * CAP * i, 2 * CAP * (i + 1))
            at = pl.ds(2 * z, 2)
            mine_rows, mine_total = rows[part].reshape(2, CAP, dim), total[part].reshape(2, CAP, LANES)
            s["rfull"][at, :, :dim] = mine_rows
            s["rhalf"][at, :, :dim] = mine_rows.astype(BF16)
            s["rfull"][at, :, dim:] = mine_total
            s["rhalf"][at, :, dim:] = split(mine_total)
            crossing.append(send(s["rhalf"].at[2 * z + 1 - core], s["sib"].at[z], sibling))

    tile = dim // 4

    def weights(n):
        cols = slice(n * tile, (n + 1) * tile)
        at = slice(n % 2 * tile, n % 2 * tile + tile)
        x_rows = jnp.concatenate([rows_at(s["xlo" if n < 2 else "xhi"], p, at) for p in range(nz)], axis=0)
        s["sums"][:, cols] = jnp.dot(s["dcat"][...], x_rows, preferred_element_type=F32)
        g_rows = jnp.concatenate([rows_at(s["glo" if n < 2 else "ghi"], p, at) for p in range(nz)], axis=0)
        s["sums_down"][:, cols] = jnp.dot(s["scaled"][...], g_rows, preferred_element_type=F32)

    sections = sections_of(dim)

    def piece(section, z):
        _, start, width, gate = section
        cols = slice(start, start + width)
        value = s["rfull"][2 * z + core, :, cols] + s["sib"][z, :, cols].astype(F32)
        if not gate:
            return value, None
        return value, s["rfull"][2 * z + core, :, dim:] + join(s["sib"][z, :, dim:])

    def add(value, ref, width):
        rows, gate_rows = value
        rows = rows + ref[:, :width].astype(F32)
        if gate_rows is not None:
            gate_rows = gate_rows + join(ref[:, width:])
        return rows, gate_rows

    crossed = set()

    def need(p):
        if p not in crossed:
            crossing[p].wait_recv()
            crossed.add(p)

    def place_of(distance):
        far = distance % nz - nz // 2
        return 2 * far if far >= 0 else -2 * far - 1

    last = {}
    for step in range(long):
        for n, section in enumerate(sections):
            hops = (long, short) if section[0] else (short, long)
            width = section[2]
            for side, sign in ((0, 1), (1, -1)):
                if step >= hops[side]:
                    continue
                if step:
                    last[n, side].wait_recv()
                distance = sign * (hops[side] - step)
                need(place_of(distance))
                value = piece(section, (mz + distance + nz) % nz)
                if step:
                    value = add(value, s[f"got{n}"].at[side, step - 1], width)
                put = s[f"put{n}"].at[side, step]
                put[:, :width] = value[0].astype(BF16)
                if section[3]:
                    put[:, width:] = split(value[1])
                last[n, side] = send(
                    put, s[f"got{n}"].at[side, step], at_z(up_z if side == 0 else down_z)
                )
        if step == 0:
            weights(0)
            weights(1)
        elif step < 3:
            weights(step + 1)
    for n in range(min(long, 3) + 1, 4):
        weights(n)
    stores = [
        pltpu.make_async_copy(s["sums"].at[pl.ds(0, units)], out_gate, s["lsem"].at[3]),
        pltpu.make_async_copy(s["sums"].at[pl.ds(units, units)], out_up, s["lsem"].at[4]),
        pltpu.make_async_copy(s["sums_down"], out_down, s["lsem"].at[5]),
    ]
    for store in stores:
        store.start()

    def back_to_tokens(place, rows):
        return lax.dot_general(place, rows, TRANSPOSED_LEFT, preferred_element_type=F32).astype(BF16)

    need(place_of(0))
    first, second = [], []
    for n, section in enumerate(sections):
        first_y, start, width, gate = section
        value = piece(section, mz)
        for side, hops in enumerate((long, short) if first_y else (short, long)):
            last[n, side].wait_recv()
            value = add(value, s[f"got{n}"].at[side, hops - 1], width)
        c, cr = s[f"c{n}"], s[f"cr{n}"]
        place = place_a if first_y else place_b
        c[:, :, :width] = back_to_tokens(place, value[0].astype(BF16)).reshape(c.shape[0], c.shape[1], width)
        if gate:
            lanes = lax.broadcasted_iota(jnp.int32, (CAP, LANES), 1)
            here = jnp.where(lanes % (LANES // 2) == mine, split(value[1]).astype(F32), 0.0).astype(BF16)
            c[:, :, width:] = back_to_tokens(place, here).reshape(c.shape[0], c.shape[1], LANES)
        if first_y:
            peers = [(my + d) % ny for d in range(1, ny)]
            first.append([send(c.at[y], cr.at[my], at_y(y)) for y in peers])
            cr[my] = c[my]
        else:
            peers = [(mx + d) % nx for d in range(1, nx)]
            first.append([send(c.at[x], cr.at[mx], at_x(x)) for x in peers])
            cr[mx] = c[mx]

    def total_of(buf):
        value = buf[0].astype(F32)
        for k in range(1, buf.shape[0]):
            value = value + buf[k].astype(F32)
        return value

    for n, section in enumerate(sections):
        arrive(first[n])
        e, er, wide = s[f"e{n}"], s[f"er{n}"], s[f"flat{n}"]
        wide[...] = total_of(s[f"cr{n}"])
        for k in range(e.shape[0]):
            e[k] = wide[2 * k : 2 * k + 2, :]
        if section[0]:
            peers = [(mx + d) % nx for d in range(1, nx)]
            second.append([send(e.at[x], er.at[mx], at_x(x)) for x in peers])
            er[mx] = e[mx]
        else:
            peers = [(my + d) % ny for d in range(1, ny)]
            second.append([send(e.at[y], er.at[my], at_y(y)) for y in peers])
            er[my] = e[my]

    for n, (_, start, width, gate) in enumerate(sections):
        arrive(second[n])
        final = total_of(s[f"er{n}"])
        out_in[:, start : start + width] = final[:, :width]
        if gate:
            grads = join(final[:, width:])
            inner = jnp.sum(spread * grads, axis=-1, keepdims=True)
            place = lax.broadcasted_iota(jnp.int32, (2, top), 1)
            result = jnp.zeros((2, top), F32)
            for k in range(top):
                own = jnp.sum(jnp.where(hits[k], grads, 0.0), axis=-1, keepdims=True)
                result = result + jnp.where(place == k, probs[:, k : k + 1] * (own - inner), 0.0)
            out_logits[...] = result
    for store in stores:
        store.wait()
    for copy in pending:
        copy.wait_send()


def hand_over(*refs):
    count = len(refs) // 2
    sources, results, sem = refs[:count], refs[count : 2 * count], refs[-1]
    copies = []
    for source, result in zip(sources, results):
        rows = source.shape[0]
        cuts = 3 if rows % 24 == 0 else 1
        for k in range(cuts):
            at = pl.ds(k * (rows // cuts), rows // cuts)
            copies.append(pltpu.make_async_copy(source.at[at], result.at[at], sem.at[len(copies)]))
    for copy in copies:
        copy.start()
    for copy in copies:
        copy.wait()


def on_device(nx, ny, nz, tokens, grad_out, expert_ids, router_logits, w_gate, w_up, w_down):
    dim, units = w_gate.shape[1], w_gate.shape[2]
    shapes = scratch_of(nx, ny, nz, dim, units)
    spec = pl.BlockSpec(memory_space=pltpu.VMEM)
    anywhere = pl.BlockSpec(memory_space=pl.ANY)
    out_shape = [
        jax.ShapeDtypeStruct((2, dim), F32),
        jax.ShapeDtypeStruct(expert_ids.shape[1:], F32),
        jax.ShapeDtypeStruct((units, dim), F32),
        jax.ShapeDtypeStruct((units, dim), F32),
        jax.ShapeDtypeStruct((units, dim), F32),
    ]
    results = pl.pallas_call(
        functools.partial(kernel, nx, ny, nz, tuple(shapes)),
        out_shape=out_shape,
        in_specs=[spec] * 4 + [anywhere] * 3,
        out_specs=[spec] * 2 + [anywhere] * 3,
        scratch_shapes=list(shapes.values()),
        compiler_params=pltpu.CompilerParams(
            collective_id=0, has_side_effects=True, vmem_limit_bytes=56 * 1024 * 1024
        ),
    )(
        tokens[0], grad_out[0], expert_ids[0], router_logits[0],
        jnp.swapaxes(w_gate[0], 0, 1), jnp.swapaxes(w_up[0], 0, 1), w_down[0],
    )
    rows, logit_grads, sum_gate, sum_up, sum_down = pl.pallas_call(
        hand_over,
        out_shape=out_shape,
        in_specs=[anywhere] * 5,
        out_specs=[anywhere] * 5,
        scratch_shapes=[pltpu.SemaphoreType.DMA((11,))],
    )(*results)
    return (
        rows[None],
        logit_grads[None],
        jnp.swapaxes(sum_gate, 0, 1)[None],
        jnp.swapaxes(sum_up, 0, 1)[None],
        sum_down[None],
    )


def solution(mesh):
    side = math.isqrt(mesh.shape["expert"])
    nz = mesh.shape["hidden"] // 2
    token_spec, wide, tall = P("hidden", "expert", None), P("expert", None, "hidden"), P("expert", "hidden", None)
    return jax.shard_map(
        functools.partial(on_device, side, side, nz),
        mesh=mesh,
        in_specs=(token_spec,) * 4 + (wide, wide, tall),
        out_specs=(token_spec, token_spec, wide, wide, tall),
        check_vma=False,
    )
```

time: 695 us -> 174 us (0.25)
  blocking collectives: 467 us -> 0 us
  waiting for transfers between devices: 183 us -> 0 us
  Pallas kernels: 0 us -> 172 us
  matrix products: 18.2 us -> 0 us
  between operations: 15.9 us -> 0.64 us
    unnamed x3 -> x0, blocking collectives: 319 us -> none
    pallas_call x0 -> x2, Pallas kernels: none -> 172 us  [the longest x1 99.1 us: on_device(): pl.pallas_call(functools.partial(kernel, nx, ny, nz, tuple(shapes)), out_...]
    unnamed x5 -> x0, waiting for transfers between devices: 170 us -> none
    all_gather x3 -> x0, blocking collectives: 148 us -> none  [the longest x1 51.4 us: on_device(): lax.all_gather(gate_table[None], 'expert', axis=1, tiled=True)]
    dot_general x13 -> x0, matrix products: 18.2 us -> none  [the longest x1 2.66 us: project_back(): lax.dot_general(d_up_pre, up_weight, (((1,), (1,)), ((), ())), preferred_...]
    all_gather x2 -> x0, waiting for transfers between devices: 12.9 us -> none  [the longest x1 12.9 us: on_device(): lax.all_gather(grad_rows, 'hidden', axis=0, tiled=True)]
  transfers between devices with their start and end apart: 4 -> 0, of which waited for: 2 -> 0; matrix products, arithmetic and copies ran while one was open for 2% -> 0% of each run, Pallas kernels for 0% -> 0%
where the time goes in v2:
time: 174 us; the launch traced here: 173 us
  Pallas kernels  172 us (99%)
    pallas_call x1, Pallas kernels, on_device(): pl.pallas_call(functools.partial(kernel, nx, ny, nz, tuple(shapes)), out_...  99.1 us
    pallas_call x1, Pallas kernels, on_device(): pl.pallas_call(hand_over, out_shape=out_shape, in_specs=[anywhere] * 5, o...  73.2 us

profile of v2, /device:TPU:14, one launch (start us, length us, event | category | flops | bytes accessed | tf_op | source)
XLA Modules:
  0.0 172.9 jit_solution(305912846144459218)
XLA Ops:
  0.6 99.1 %shard_map.110 = (f32[2,2048]{1,0:T(2,128)}, f32[2,8]{1,0:T(2,128)}, f32[96,2048]{1,0:T(8,128)}, f32[96,2048]{1,0:T(8,128)}, f32[96,2048]{1,0:T(8,128)}) custom-call(bf16[2,2048]{1,0:T(2,128)(2,1)} %bitcast.23, bf16[2,2048]{1,0:T(2,128)(2,1)} %bitcast.24, s32[2,8]{1,0:T(2,128)} %bitcast.25, f32[2,8]{1,0:T(2,128)} %bitcast.26, bf16[96,2048]{1,0:T(8,128)(2,1)} %bitcast.20, ...), custom_call_target="tpu_custom_call" | custom-call | tf_op jit(solution)/shard_map/pallas_call | solution.py:487
  99.7 73.2 %shard_map.111 = (f32[2,2048]{1,0:T(2,128)}, f32[2,8]{1,0:T(2,128)}, f32[96,2048]{1,0:T(8,128)}, f32[96,2048]{1,0:T(8,128)}, f32[96,2048]{1,0:T(8,128)}) custom-call(f32[2,2048]{1,0:T(2,128)} %get-tuple-element.15.refs_0_, f32[2,8]{1,0:T(2,128)} %get-tuple-element.16.refs_1_, f32[96,2048]{1,0:T(8,128)} %get-tuple-element.17.refs_2_, ...), custom_call_target="tpu_custom_call" | custom-call | tf_op jit(solution)/shard_map/pallas_call | solution.py:500

commit v3 on v2

--- a/solution.py
+++ b/solution.py
@@ -166,18 +166,53 @@
             wide[2 * k : 2 * k + 2, :width] = blocks[k].astype(F32)
         return wide[:, :width].astype(BF16)
 
+    def ring_start(buf, at, place, size, hops, up, down, across):
+        own = buf.at[at(place)]
+        waits = [send(own, own, device) if hop else None for hop, device in zip(hops, (up, down))]
+        over = {0: send(own, own, sibling)} if across else {}
+        return buf, at, place, size, hops, (up, down), waits, over, across
+
+    def ring_step(ring, step):
+        buf, at, place, size, hops, devices, waits, over, across = ring
+        for side in (0, 1) if hops[0] >= hops[1] else (1, 0):
+            if step >= hops[side]:
+                continue
+            distance = -(step + 1) if side == 0 else step + 1
+            waits[side].wait_recv()
+            block = buf.at[at((place + distance + size) % size)]
+            if step + 1 < hops[side]:
+                waits[side] = send(block, block, devices[side])
+            if across:
+                over[distance % size] = send(block, block, sibling)
+
+    def ring_x(buf, hops):
+        return ring_start(buf, lambda x: x, mx, nx, hops, at_x((mx + 1) % nx), at_x((mx + nx - 1) % nx), False)
+
+    def ring_y(buf, hops):
+        return ring_start(buf, lambda y: y, my, ny, hops, at_y((my + 1) % ny), at_y((my + ny - 1) % ny), False)
+
+    def ring_z(buf, hops):
+        return ring_start(buf, lambda z: 2 * z + core, mz, nz, hops, at_z(up_z), at_z(down_z), True)
+
+    def ways(size):
+        return size // 2, size - 1 - size // 2
+
     arrive(xa)
     s["xa2"][my] = flatten(s["xa1"], s["flat_a"])
-    xa = spread_y(s["xa2"].at[my], s["xa2"])
+    xa = ring_y(s["xa2"], ways(ny))
     arrive(xb)
     s["xb2"][mx] = flatten(s["xb1"], s["flat_b"])
-    xb = spread_x(s["xb2"].at[mx], s["xb2"])
+    xb = ring_x(s["xb2"], ways(nx))
     arrive(ga)
     s["ga2"][my] = flatten(s["ga1"], s["flat_a"])
-    ga = spread_y(s["ga2"].at[my], s["ga2"])
+    ga = ring_y(s["ga2"], ways(ny)[::-1])
     arrive(gb)
     s["gb2"][mx] = flatten(s["gb1"], s["flat_b"])
-    gb = spread_x(s["gb2"].at[mx], s["gb2"])
+    gb = ring_x(s["gb2"], ways(nx)[::-1])
+    last_step = max(nx, ny) // 2 - 1
+    for step in range(last_step):
+        for ring in (xa, xb, ga, gb):
+            ring_step(ring, step)
 
     own_lane = jnp.where(lax.broadcasted_iota(jnp.int32, (8, LANES), 1) == mine, 1.0, 0.0).astype(BF16)
 
@@ -199,50 +234,33 @@
         slot = lax.broadcasted_iota(jnp.int32, (CAP, tokens), 0).astype(F32)
         return jnp.where(rank[0:1, :] == slot, 1.0, 0.0).astype(BF16)
 
-    def ring_start(buf, hops):
-        own = buf.at[hid]
-        waits = [send(own, own, at_z(up_z)), send(own, own, at_z(down_z))]
-        return buf, hops, waits, [send(own, own, sibling)]
-
-    def ring_step(ring, step):
-        buf, hops, waits, over = ring
-        for side, sign in ((0, 1), (1, -1)) if hops[0] >= hops[1] else ((1, -1), (0, 1)):
-            if step >= hops[side]:
-                continue
-            waits[side].wait_recv()
-            block = buf.at[2 * ((mz - sign * (step + 1) + nz) % nz) + core]
-            if step + 1 < hops[side]:
-                waits[side] = send(block, block, at_z(up_z if side == 0 else down_z))
-            over.append(send(block, block, sibling))
-
-    arrive(xa)
+    ring_step(xa, last_step)
     wide_a = s["xa2"][...].reshape(tokens, half + LANES)
     place_a = placing_of(wide_a[:, half:], order_a)
     s["xlo"][hid] = jnp.dot(place_a, wide_a[:, :half], preferred_element_type=F32).astype(BF16)
-    x_low = ring_start(s["xlo"], (long, short))
-    arrive(xb)
+    x_low = ring_z(s["xlo"], (long, short))
+    ring_step(xb, last_step)
     wide_b = s["xb2"][...].reshape(tokens, half + LANES)
     place_b = placing_of(wide_b[:, half:], order_b)
     s["xhi"][hid] = jnp.dot(place_b, wide_b, preferred_element_type=F32).astype(BF16)
-    x_high = ring_start(s["xhi"], (short, long))
-    ring_step(x_low, 0)
-    ring_step(x_high, 0)
-    arrive(ga)
+    x_high = ring_z(s["xhi"], (short, long))
+    ring_step(ga, last_step)
     s["glo"][hid] = jnp.dot(
         place_a, s["ga2"][...].reshape(tokens, half), preferred_element_type=F32
     ).astype(BF16)
-    g_low = ring_start(s["glo"], (long, short))
-    arrive(gb)
+    g_low = ring_z(s["glo"], (long, short))
+    ring_step(gb, last_step)
     s["ghi"][hid] = jnp.dot(
         place_b, s["gb2"][...].reshape(tokens, half), preferred_element_type=F32
     ).astype(BF16)
-    g_high = ring_start(s["ghi"], (short, long))
-    for step in range(1, long):
+    g_high = ring_z(s["ghi"], (short, long))
+    for step in range(long):
         ring_step(x_low, step)
         ring_step(x_high, step)
-        ring_step(g_low, step - 1)
-        ring_step(g_high, step - 1)
-    arrive(x_low[3] + x_high[3])
+        if step + 1 < long:
+            ring_step(g_low, step)
+            ring_step(g_high, step)
+    arrive(list(x_low[7].values()) + list(x_high[7].values()))
 
     def z_at(p):
         step = (p + 1) // 2
@@ -275,12 +293,14 @@
 
     groups = nz // pair
     lax.fori_loop(0, groups, forward, 0)
-    ring_step(g_low, long - 1)
-    ring_step(g_high, long - 1)
-    arrive(g_low[3] + g_high[3])
-
-    crossing = []
-    for g in range(groups):
+    crossing = {}
+    for g in range(groups - 1, -1, -1):
+        if g == 0:
+            ring_step(g_low, long - 1)
+            ring_step(g_high, long - 1)
+        for p in range(g * pair, (g + 1) * pair):
+            distance = (nz // 2 + (1 - 2 * (p % 2)) * ((p + 1) // 2)) % nz
+            arrive([g_low[7][distance], g_high[7][distance]])
         cols = slice(g * LANES, (g + 1) * LANES)
         back = lax.dot_general(
             s["wd"][:, low], rows_of(s["glo"], g, every), TRANSPOSED_RIGHT, preferred_element_type=F32
@@ -312,7 +332,7 @@
             s["rhalf"][at, :, :dim] = mine_rows.astype(BF16)
             s["rfull"][at, :, dim:] = mine_total
             s["rhalf"][at, :, dim:] = split(mine_total)
-            crossing.append(send(s["rhalf"].at[2 * z + 1 - core], s["sib"].at[z], sibling))
+            crossing[g * pair + i] = send(s["rhalf"].at[2 * z + 1 - core], s["sib"].at[z], sibling)
 
     tile = dim // 4
 
@@ -457,19 +477,24 @@
 
 
 def hand_over(*refs):
-    count = len(refs) // 2
-    sources, results, sem = refs[:count], refs[count : 2 * count], refs[-1]
-    copies = []
-    for source, result in zip(sources, results):
+    count = 5
+    sources, results, stages = refs[:count], refs[count : 2 * count], refs[2 * count : 3 * count]
+    load_sem, store_sem = refs[-2:]
+    loads, stores = [], []
+    for source, result, stage in zip(sources, results, stages):
         rows = source.shape[0]
         cuts = 3 if rows % 24 == 0 else 1
         for k in range(cuts):
-            at = pl.ds(k * (rows // cuts), rows // cuts)
-            copies.append(pltpu.make_async_copy(source.at[at], result.at[at], sem.at[len(copies)]))
-    for copy in copies:
-        copy.start()
-    for copy in copies:
-        copy.wait()
+            at, number = pl.ds(k * (rows // cuts), rows // cuts), len(loads)
+            loads.append(pltpu.make_async_copy(source.at[at], stage.at[at], load_sem.at[number]))
+            stores.append(pltpu.make_async_copy(stage.at[at], result.at[at], store_sem.at[number]))
+    for load in loads:
+        load.start()
+    for load, store in zip(loads, stores):
+        load.wait()
+        store.start()
+    for store in stores:
+        store.wait()
 
 
 def on_device(nx, ny, nz, tokens, grad_out, expert_ids, router_logits, w_gate, w_up, w_down):
@@ -502,7 +527,8 @@
         out_shape=out_shape,
         in_specs=[anywhere] * 5,
         out_specs=[anywhere] * 5,
-        scratch_shapes=[pltpu.SemaphoreType.DMA((11,))],
+        scratch_shapes=[pltpu.VMEM(one.shape, F32) for one in out_shape]
+        + [pltpu.SemaphoreType.DMA((11,))] * 2,
     )(*results)
     return (
         rows[None],

time: 174 us -> 106 us (0.61)
  Pallas kernels: 172 us -> 105 us
    pallas_call x1, Pallas kernels: 73.2 us -> 2.56 us  [on_device(): pl.pallas_call(hand_over, out_shape=out_shape, in_specs=[anywhere] * 5, o...]
    pallas_call x1, Pallas kernels: 99.1 us -> 102 us  [on_device(): pl.pallas_call(functools.partial(kernel, nx, ny, nz, tuple(shapes)), out_...]
where the time goes in v3:
time: 106 us; the launch traced here: 105 us
  Pallas kernels  105 us (99%)
    pallas_call x1, Pallas kernels, on_device(): pl.pallas_call(functools.partial(kernel, nx, ny, nz, tuple(shapes)), out_...  102 us
    pallas_call x1, Pallas kernels, on_device(): pl.pallas_call(hand_over, out_shape=out_shape, in_specs=[anywhere] * 5, o...  2.56 us

profile of v3, /device:TPU:14, one launch (start us, length us, event | category | flops | bytes accessed | tf_op | source)
XLA Modules:
  0.0 105.4 jit_solution(15542682520383877256)
XLA Ops:
  0.6 102.2 %shard_map.110 = (f32[2,2048]{1,0:T(2,128)}, f32[2,8]{1,0:T(2,128)}, f32[96,2048]{1,0:T(8,128)}, f32[96,2048]{1,0:T(8,128)}, f32[96,2048]{1,0:T(8,128)}) custom-call(bf16[2,2048]{1,0:T(2,128)(2,1)} %bitcast.23, bf16[2,2048]{1,0:T(2,128)(2,1)} %bitcast.24, s32[2,8]{1,0:T(2,128)} %bitcast.25, f32[2,8]{1,0:T(2,128)} %bitcast.26, bf16[96,2048]{1,0:T(8,128)(2,1)} %bitcast.20, ...), custom_call_target="tpu_custom_call" | custom-call | tf_op jit(solution)/shard_map/pallas_call | solution.py:512
  102.8 2.6 %shard_map.111 = (f32[2,2048]{1,0:T(2,128)}, f32[2,8]{1,0:T(2,128)}, f32[96,2048]{1,0:T(8,128)}, f32[96,2048]{1,0:T(8,128)}, f32[96,2048]{1,0:T(8,128)}) custom-call(f32[2,2048]{1,0:T(2,128)} %get-tuple-element.15.refs_0_, f32[2,8]{1,0:T(2,128)} %get-tuple-element.16.refs_1_, f32[96,2048]{1,0:T(8,128)} %get-tuple-element.17.refs_2_, ...), custom_call_target="tpu_custom_call" | custom-call | tf_op jit(solution)/shard_map/pallas_call | solution.py:525

commit v4 on v3

--- a/solution.py
+++ b/solution.py
@@ -53,7 +53,6 @@
         "xlo": vmem((2 * nz, CAP, half), BF16), "xhi": vmem((2 * nz, CAP, wide), BF16),
         "glo": vmem((2 * nz, CAP, half), BF16), "ghi": vmem((2 * nz, CAP, half), BF16),
         "wgu": vmem((2 * units, dim), BF16), "wd": vmem((units, dim), BF16),
-        "pre": vmem((2 * units, flat), F32), "weight": vmem((8, flat), F32),
         "dcat": vmem((2 * units, flat), BF16), "scaled": vmem((units, flat), BF16),
         "rfull": vmem((2 * nz, CAP, padded), F32), "rhalf": vmem((2 * nz, CAP, padded), BF16),
         "sib": vmem((nz, CAP, padded), BF16),
@@ -153,10 +152,10 @@
 
     xa = spread_x(s["xa"], s["xa1"])
     xb = spread_y(s["xb"], s["xb1"])
+    ga = spread_x(grd.at[:, pl.ds(0, half)], s["ga1"])
+    gb = spread_y(grd.at[:, pl.ds(half, half)], s["gb1"])
     s["xa1"][mx] = s["xa"][...]
     s["xb1"][my] = s["xb"][...]
-    ga = spread_x(grd.at[:, pl.ds(0, half)], s["ga1"])
-    gb = spread_y(grd.at[:, pl.ds(half, half)], s["gb1"])
     s["ga1"][mx] = grd[:, :half]
     s["gb1"][my] = grd[:, half:]
 
@@ -185,34 +184,40 @@
             if across:
                 over[distance % size] = send(block, block, sibling)
 
-    def ring_x(buf, hops):
-        return ring_start(buf, lambda x: x, mx, nx, hops, at_x((mx + 1) % nx), at_x((mx + nx - 1) % nx), False)
-
-    def ring_y(buf, hops):
-        return ring_start(buf, lambda y: y, my, ny, hops, at_y((my + 1) % ny), at_y((my + ny - 1) % ny), False)
-
     def ring_z(buf, hops):
         return ring_start(buf, lambda z: 2 * z + core, mz, nz, hops, at_z(up_z), at_z(down_z), True)
 
-    def ways(size):
-        return size // 2, size - 1 - size // 2
-
+    def hand_start(buf, at, size, device):
+        own = buf.at[at]
+        far = range(1, size) if size != 8 else (2, 6, 1, 7)
+        return {-d % size: send(own, own, device((at + d) % size)) for d in far}
+
+    def hand_on(copies, buf, at, size, device, upward):
+        if size != 8:
+            return
+        for toward in (1, -1):
+            from_here = -2 * toward % size
+            copies.pop(from_here).wait_recv()
+            block = buf.at[(at - 2 * toward + size) % size]
+            copies[-3 * toward % size] = send(block, block, device((at + toward + size) % size))
+            if (toward > 0) == upward:
+                copies[4] = send(block, block, device((at + 2 * toward + size) % size))
+
+    along_y, along_x = (my, ny, at_y), (mx, nx, at_x)
     arrive(xa)
     s["xa2"][my] = flatten(s["xa1"], s["flat_a"])
-    xa = ring_y(s["xa2"], ways(ny))
+    xa = hand_start(s["xa2"], *along_y)
     arrive(xb)
     s["xb2"][mx] = flatten(s["xb1"], s["flat_b"])
-    xb = ring_x(s["xb2"], ways(nx))
+    xb = hand_start(s["xb2"], *along_x)
     arrive(ga)
     s["ga2"][my] = flatten(s["ga1"], s["flat_a"])
-    ga = ring_y(s["ga2"], ways(ny)[::-1])
     arrive(gb)
     s["gb2"][mx] = flatten(s["gb1"], s["flat_b"])
-    gb = ring_x(s["gb2"], ways(nx)[::-1])
-    last_step = max(nx, ny) // 2 - 1
-    for step in range(last_step):
-        for ring in (xa, xb, ga, gb):
-            ring_step(ring, step)
+    hand_on(xa, s["xa2"], *along_y, True)
+    hand_on(xb, s["xb2"], *along_x, True)
+    ga = hand_start(s["ga2"], *along_y)
+    gb = hand_start(s["gb2"], *along_x)
 
     own_lane = jnp.where(lax.broadcasted_iota(jnp.int32, (8, LANES), 1) == mine, 1.0, 0.0).astype(BF16)
 
@@ -234,34 +239,28 @@
         slot = lax.broadcasted_iota(jnp.int32, (CAP, tokens), 0).astype(F32)
         return jnp.where(rank[0:1, :] == slot, 1.0, 0.0).astype(BF16)
 
-    ring_step(xa, last_step)
+    arrive(xa.values())
     wide_a = s["xa2"][...].reshape(tokens, half + LANES)
     place_a = placing_of(wide_a[:, half:], order_a)
     s["xlo"][hid] = jnp.dot(place_a, wide_a[:, :half], preferred_element_type=F32).astype(BF16)
     x_low = ring_z(s["xlo"], (long, short))
-    ring_step(xb, last_step)
+    arrive(xb.values())
     wide_b = s["xb2"][...].reshape(tokens, half + LANES)
     place_b = placing_of(wide_b[:, half:], order_b)
     s["xhi"][hid] = jnp.dot(place_b, wide_b, preferred_element_type=F32).astype(BF16)
     x_high = ring_z(s["xhi"], (short, long))
-    ring_step(ga, last_step)
+    hand_on(ga, s["ga2"], *along_y, False)
+    hand_on(gb, s["gb2"], *along_x, False)
+    arrive(ga.values())
     s["glo"][hid] = jnp.dot(
         place_a, s["ga2"][...].reshape(tokens, half), preferred_element_type=F32
     ).astype(BF16)
     g_low = ring_z(s["glo"], (long, short))
-    ring_step(gb, last_step)
+    arrive(gb.values())
     s["ghi"][hid] = jnp.dot(
         place_b, s["gb2"][...].reshape(tokens, half), preferred_element_type=F32
     ).astype(BF16)
     g_high = ring_z(s["ghi"], (short, long))
-    for step in range(long):
-        ring_step(x_low, step)
-        ring_step(x_high, step)
-        if step + 1 < long:
-            ring_step(g_low, step)
-            ring_step(g_high, step)
-    arrive(list(x_low[7].values()) + list(x_high[7].values()))
-
     def z_at(p):
         step = (p + 1) // 2
         return (mz + nz // 2 + (1 - 2 * (p % 2)) * step + nz) % nz
@@ -274,41 +273,30 @@
     def rows_of(buf, g, columns):
         return jnp.concatenate([rows_at(buf, g * pair + i, columns) for i in range(pair)], axis=0)
 
-    for load in loads:
-        load.wait()
     every, low, high = slice(None), slice(0, half), slice(half, dim)
-
-    def forward(g, _):
-        cols = pl.ds(pl.multiple_of(g * LANES, LANES), LANES)
+    groups = nz // pair
+    crossing = {}
+
+    def compute(g):
+        for p in range(g * pair, (g + 1) * pair):
+            distance = (nz // 2 + (1 - 2 * (p % 2)) * ((p + 1) // 2)) % nz
+            arrive([ring[7][distance] for ring in (x_low, x_high, g_low, g_high)])
+        cols = slice(g * LANES, (g + 1) * LANES)
         x_hi = rows_of(s["xhi"], g, every)
-        s["pre"][:, cols] = lax.dot_general(
+        pre = lax.dot_general(
             s["wgu"][:, low], rows_of(s["xlo"], g, every), TRANSPOSED_RIGHT, preferred_element_type=F32
         ) + lax.dot_general(
             s["wgu"][:, high], x_hi[:, :half], TRANSPOSED_RIGHT, preferred_element_type=F32
         )
-        s["weight"][:, cols] = lax.dot_general(
+        weight = lax.dot_general(
             own_lane, x_hi[:, half:], TRANSPOSED_RIGHT, preferred_element_type=F32
-        )
-        return 0
-
-    groups = nz // pair
-    lax.fori_loop(0, groups, forward, 0)
-    crossing = {}
-    for g in range(groups - 1, -1, -1):
-        if g == 0:
-            ring_step(g_low, long - 1)
-            ring_step(g_high, long - 1)
-        for p in range(g * pair, (g + 1) * pair):
-            distance = (nz // 2 + (1 - 2 * (p % 2)) * ((p + 1) // 2)) % nz
-            arrive([g_low[7][distance], g_high[7][distance]])
-        cols = slice(g * LANES, (g + 1) * LANES)
+        )[0:1, :]
         back = lax.dot_general(
             s["wd"][:, low], rows_of(s["glo"], g, every), TRANSPOSED_RIGHT, preferred_element_type=F32
         ) + lax.dot_general(
             s["wd"][:, high], rows_of(s["ghi"], g, every), TRANSPOSED_RIGHT, preferred_element_type=F32
         )
-        pre_gate, pre_up = s["pre"][:units, cols], s["pre"][units:, cols]
-        weight = s["weight"][0:1, cols]
+        pre_gate, pre_up = pre[:units], pre[units:]
         sigmoid = 1.0 / (1.0 + jnp.exp(-pre_gate))
         silu = pre_gate * sigmoid
         active = silu * pre_up
@@ -334,6 +322,18 @@
             s["rhalf"][at, :, dim:] = split(mine_total)
             crossing[g * pair + i] = send(s["rhalf"].at[2 * z + 1 - core], s["sib"].at[z], sibling)
 
+    for load in loads:
+        load.wait()
+    for step in range(long):
+        ring_step(x_low, step)
+        ring_step(x_high, step)
+        ring_step(g_low, step)
+        ring_step(g_high, step)
+        if step >= 1:
+            compute(groups - step)
+    for g in range(groups - long, -1, -1):
+        compute(g)
+
     tile = dim // 4
 
     def weights(n):
@@ -372,54 +372,41 @@
         far = distance % nz - nz // 2
         return 2 * far if far >= 0 else -2 * far - 1
 
-    last = {}
-    for step in range(long):
-        for n, section in enumerate(sections):
-            hops = (long, short) if section[0] else (short, long)
-            width = section[2]
-            for side, sign in ((0, 1), (1, -1)):
-                if step >= hops[side]:
-                    continue
-                if step:
-                    last[n, side].wait_recv()
-                distance = sign * (hops[side] - step)
-                need(place_of(distance))
-                value = piece(section, (mz + distance + nz) % nz)
-                if step:
-                    value = add(value, s[f"got{n}"].at[side, step - 1], width)
-                put = s[f"put{n}"].at[side, step]
-                put[:, :width] = value[0].astype(BF16)
-                if section[3]:
-                    put[:, width:] = split(value[1])
-                last[n, side] = send(
-                    put, s[f"got{n}"].at[side, step], at_z(up_z if side == 0 else down_z)
-                )
-        if step == 0:
-            weights(0)
-            weights(1)
-        elif step < 3:
-            weights(step + 1)
-    for n in range(min(long, 3) + 1, 4):
-        weights(n)
-    stores = [
-        pltpu.make_async_copy(s["sums"].at[pl.ds(0, units)], out_gate, s["lsem"].at[3]),
-        pltpu.make_async_copy(s["sums"].at[pl.ds(units, units)], out_up, s["lsem"].at[4]),
-        pltpu.make_async_copy(s["sums_down"], out_down, s["lsem"].at[5]),
-    ]
-    for store in stores:
-        store.start()
+    last, first, second = {}, {}, {}
+
+    def reduce_step(n, step):
+        section = sections[n]
+        hops = (long, short) if section[0] else (short, long)
+        width = section[2]
+        for side, sign in ((0, 1), (1, -1)):
+            if step >= hops[side]:
+                continue
+            if step:
+                last[n, side].wait_recv()
+            distance = sign * (hops[side] - step)
+            need(place_of(distance))
+            value = piece(section, (mz + distance + nz) % nz)
+            if step:
+                value = add(value, s[f"got{n}"].at[side, step - 1], width)
+            put = s[f"put{n}"].at[side, step]
+            put[:, :width] = value[0].astype(BF16)
+            if section[3]:
+                put[:, width:] = split(value[1])
+            last[n, side] = send(
+                put, s[f"got{n}"].at[side, step], at_z(up_z if side == 0 else down_z)
+            )
 
     def back_to_tokens(place, rows):
         return lax.dot_general(place, rows, TRANSPOSED_LEFT, preferred_element_type=F32).astype(BF16)
 
-    need(place_of(0))
-    first, second = [], []
-    for n, section in enumerate(sections):
-        first_y, start, width, gate = section
+    def reduce_end(n):
+        first_y, start, width, gate = section = sections[n]
+        need(place_of(0))
         value = piece(section, mz)
         for side, hops in enumerate((long, short) if first_y else (short, long)):
-            last[n, side].wait_recv()
-            value = add(value, s[f"got{n}"].at[side, hops - 1], width)
+            if hops:
+                last[n, side].wait_recv()
+                value = add(value, s[f"got{n}"].at[side, hops - 1], width)
         c, cr = s[f"c{n}"], s[f"cr{n}"]
         place = place_a if first_y else place_b
         c[:, :, :width] = back_to_tokens(place, value[0].astype(BF16)).reshape(c.shape[0], c.shape[1], width)
@@ -428,13 +415,32 @@
             here = jnp.where(lanes % (LANES // 2) == mine, split(value[1]).astype(F32), 0.0).astype(BF16)
             c[:, :, width:] = back_to_tokens(place, here).reshape(c.shape[0], c.shape[1], LANES)
         if first_y:
-            peers = [(my + d) % ny for d in range(1, ny)]
-            first.append([send(c.at[y], cr.at[my], at_y(y)) for y in peers])
+            peers = [(my + d) % ny for d in sorted(range(1, ny), key=lambda d: -min(d, ny - d))]
+            first[n] = [send(c.at[y], cr.at[my], at_y(y)) for y in peers]
             cr[my] = c[my]
         else:
-            peers = [(mx + d) % nx for d in range(1, nx)]
-            first.append([send(c.at[x], cr.at[mx], at_x(x)) for x in peers])
+            peers = [(mx + d) % nx for d in sorted(range(1, nx), key=lambda d: -min(d, nx - d))]
+            first[n] = [send(c.at[x], cr.at[mx], at_x(x)) for x in peers]
             cr[mx] = c[mx]
+
+    for turn in range(long + 1):
+        for n in range(len(sections)):
+            if turn < long:
+                reduce_step(n, turn)
+            else:
+                reduce_end(n)
+        if turn < 4:
+            weights(turn)
+        if turn == min(3, long):
+            for n in range(turn + 1, 4):
+                weights(n)
+            stores = [
+                pltpu.make_async_copy(s["sums"].at[pl.ds(0, units)], out_gate, s["lsem"].at[3]),
+                pltpu.make_async_copy(s["sums"].at[pl.ds(units, units)], out_up, s["lsem"].at[4]),
+                pltpu.make_async_copy(s["sums_down"], out_down, s["lsem"].at[5]),
+            ]
+            for store in stores:
+                store.start()
 
     def total_of(buf):
         value = buf[0].astype(F32)
@@ -449,12 +455,12 @@
         for k in range(e.shape[0]):
             e[k] = wide[2 * k : 2 * k + 2, :]
         if section[0]:
-            peers = [(mx + d) % nx for d in range(1, nx)]
-            second.append([send(e.at[x], er.at[mx], at_x(x)) for x in peers])
+            peers = [(mx + d) % nx for d in sorted(range(1, nx), key=lambda d: -min(d, nx - d))]
+            second[n] = [send(e.at[x], er.at[mx], at_x(x)) for x in peers]
             er[mx] = e[mx]
         else:
-            peers = [(my + d) % ny for d in range(1, ny)]
-            second.append([send(e.at[y], er.at[my], at_y(y)) for y in peers])
+            peers = [(my + d) % ny for d in sorted(range(1, ny), key=lambda d: -min(d, ny - d))]
+            second[n] = [send(e.at[y], er.at[my], at_y(y)) for y in peers]
             er[my] = e[my]
 
     for n, (_, start, width, gate) in enumerate(sections):

time: 106 us -> 99.4 us (0.938)
  Pallas kernels: 105 us -> 98.5 us
    pallas_call x1, Pallas kernels: 102 us -> 96 us  [on_device(): pl.pallas_call(functools.partial(kernel, nx, ny, nz, tuple(shapes)), out_...]
where the time goes in v4:
time: 99.4 us; the launch traced here: 99.2 us
  Pallas kernels  98.5 us (99%)
    pallas_call x1, Pallas kernels, on_device(): pl.pallas_call(functools.partial(kernel, nx, ny, nz, tuple(shapes)), out_...  96 us
    pallas_call x1, Pallas kernels, on_device(): pl.pallas_call(hand_over, out_shape=out_shape, in_specs=[anywhere] * 5, o...  2.56 us

profile of v4, /device:TPU:14, one launch (start us, length us, event | category | flops | bytes accessed | tf_op | source)
XLA Modules:
  0.0 99.2 jit_solution(16233202570807356151)
XLA Ops:
  0.6 96.0 %shard_map.110 = (f32[2,2048]{1,0:T(2,128)}, f32[2,8]{1,0:T(2,128)}, f32[96,2048]{1,0:T(8,128)}, f32[96,2048]{1,0:T(8,128)}, f32[96,2048]{1,0:T(8,128)}) custom-call(bf16[2,2048]{1,0:T(2,128)(2,1)} %bitcast.23, bf16[2,2048]{1,0:T(2,128)(2,1)} %bitcast.24, s32[2,8]{1,0:T(2,128)} %bitcast.25, f32[2,8]{1,0:T(2,128)} %bitcast.26, bf16[96,2048]{1,0:T(8,128)(2,1)} %bitcast.20, ...), custom_call_target="tpu_custom_call" | custom-call | tf_op jit(solution)/shard_map/pallas_call | solution.py:518
  96.6 2.6 %shard_map.111 = (f32[2,2048]{1,0:T(2,128)}, f32[2,8]{1,0:T(2,128)}, f32[96,2048]{1,0:T(8,128)}, f32[96,2048]{1,0:T(8,128)}, f32[96,2048]{1,0:T(8,128)}) custom-call(f32[2,2048]{1,0:T(2,128)} %get-tuple-element.15.refs_0_, f32[2,8]{1,0:T(2,128)} %get-tuple-element.16.refs_1_, f32[96,2048]{1,0:T(8,128)} %get-tuple-element.17.refs_2_, ...), custom_call_target="tpu_custom_call" | custom-call | tf_op jit(solution)/shard_map/pallas_call | solution.py:531

commit v5 on v4

--- a/solution.py
+++ b/solution.py
@@ -44,10 +44,9 @@
     wide = half + LANES
     flat = 2 * nz * CAP
     shapes = {
-        "xa": vmem((2, wide), BF16), "xb": vmem((2, wide), BF16),
-        "xa1": vmem((nx, 2, wide), BF16), "xb1": vmem((ny, 2, wide), BF16),
-        "ga1": vmem((nx, 2, half), BF16), "gb1": vmem((ny, 2, half), BF16),
-        "flat_a": vmem((2 * nx, wide), F32), "flat_b": vmem((2 * ny, wide), F32),
+        "xa": vmem((2, padded), BF16), "xb": vmem((2, padded), BF16),
+        "xa1": vmem((nx, 2, padded), BF16), "xb1": vmem((ny, 2, padded), BF16),
+        "flat_a": vmem((2 * nx, padded), F32), "flat_b": vmem((2 * ny, padded), F32),
         "xa2": vmem((ny, 2 * nx, wide), BF16), "xb2": vmem((nx, 2 * ny, wide), BF16),
         "ga2": vmem((ny, 2 * nx, half), BF16), "gb2": vmem((nx, 2 * ny, half), BF16),
         "xlo": vmem((2 * nz, CAP, half), BF16), "xhi": vmem((2 * nz, CAP, wide), BF16),
@@ -85,6 +84,7 @@
     units, dim = wdn.shape
     top = ids.shape[1]
     half = dim // 2
+    wide = half + LANES
     tokens = 2 * nx * ny
     long, short = nz // 2, nz // 2 - 1
 
@@ -140,8 +140,10 @@
     table = spread.astype(BF16)
     s["xa"][:, :half] = tok[:, :half]
     s["xb"][:, :half] = tok[:, half:]
-    s["xa"][:, half:] = table
-    s["xb"][:, half:] = table
+    s["xa"][:, half:wide] = table
+    s["xb"][:, half:wide] = table
+    s["xa"][:, wide:] = grd[:, :half]
+    s["xb"][:, wide:] = grd[:, half:]
     pl.semaphore_wait(barrier, len(greet))
 
     def spread_x(src, dst):
@@ -152,18 +154,13 @@
 
     xa = spread_x(s["xa"], s["xa1"])
     xb = spread_y(s["xb"], s["xb1"])
-    ga = spread_x(grd.at[:, pl.ds(0, half)], s["ga1"])
-    gb = spread_y(grd.at[:, pl.ds(half, half)], s["gb1"])
     s["xa1"][mx] = s["xa"][...]
     s["xb1"][my] = s["xb"][...]
-    s["ga1"][mx] = grd[:, :half]
-    s["gb1"][my] = grd[:, half:]
-
-    def flatten(blocks, wide):
-        count, _, width = blocks.shape
-        for k in range(count):
-            wide[2 * k : 2 * k + 2, :width] = blocks[k].astype(F32)
-        return wide[:, :width].astype(BF16)
+
+    def flatten(blocks, flat):
+        for k in range(blocks.shape[0]):
+            flat[2 * k : 2 * k + 2, :] = blocks[k].astype(F32)
+        return flat[...].astype(BF16)
 
     def ring_start(buf, at, place, size, hops, up, down, across):
         own = buf.at[at(place)]
@@ -205,15 +202,15 @@
 
     along_y, along_x = (my, ny, at_y), (mx, nx, at_x)
     arrive(xa)
-    s["xa2"][my] = flatten(s["xa1"], s["flat_a"])
+    flat = flatten(s["xa1"], s["flat_a"])
+    s["xa2"][my] = flat[:, :wide]
+    s["ga2"][my] = flat[:, wide:]
     xa = hand_start(s["xa2"], *along_y)
     arrive(xb)
-    s["xb2"][mx] = flatten(s["xb1"], s["flat_b"])
+    flat = flatten(s["xb1"], s["flat_b"])
+    s["xb2"][mx] = flat[:, :wide]
+    s["gb2"][mx] = flat[:, wide:]
     xb = hand_start(s["xb2"], *along_x)
-    arrive(ga)
-    s["ga2"][my] = flatten(s["ga1"], s["flat_a"])
-    arrive(gb)
-    s["gb2"][mx] = flatten(s["gb1"], s["flat_b"])
     hand_on(xa, s["xa2"], *along_y, True)
     hand_on(xb, s["xb2"], *along_x, True)
     ga = hand_start(s["ga2"], *along_y)
@@ -251,6 +248,8 @@
     x_high = ring_z(s["xhi"], (short, long))
     hand_on(ga, s["ga2"], *along_y, False)
     hand_on(gb, s["gb2"], *along_x, False)
+    ring_step(x_low, 0)
+    ring_step(x_high, 0)
     arrive(ga.values())
     s["glo"][hid] = jnp.dot(
         place_a, s["ga2"][...].reshape(tokens, half), preferred_element_type=F32
@@ -324,15 +323,17 @@
 
     for load in loads:
         load.wait()
-    for step in range(long):
+    for step in range(1, long):
         ring_step(x_low, step)
         ring_step(x_high, step)
-        ring_step(g_low, step)
-        ring_step(g_high, step)
-        if step >= 1:
-            compute(groups - step)
-    for g in range(groups - long, -1, -1):
-        compute(g)
+        ring_step(g_low, step - 1)
+        ring_step(g_high, step - 1)
+        if step >= 2:
+            compute(groups + 1 - step)
+    compute(1)
+    ring_step(g_low, long - 1)
+    ring_step(g_high, long - 1)
+    compute(0)
 
     tile = dim // 4
 
@@ -489,7 +490,7 @@
     loads, stores = [], []
     for source, result, stage in zip(sources, results, stages):
         rows = source.shape[0]
-        cuts = 3 if rows % 24 == 0 else 1
+        cuts = 6 if rows % 48 == 0 else 1
         for k in range(cuts):
             at, number = pl.ds(k * (rows // cuts), rows // cuts), len(loads)
             loads.append(pltpu.make_async_copy(source.at[at], stage.at[at], load_sem.at[number]))
@@ -534,7 +535,7 @@
         in_specs=[anywhere] * 5,
         out_specs=[anywhere] * 5,
         scratch_shapes=[pltpu.VMEM(one.shape, F32) for one in out_shape]
-        + [pltpu.SemaphoreType.DMA((11,))] * 2,
+        + [pltpu.SemaphoreType.DMA((20,))] * 2,
     )(*results)
     return (
         rows[None],

time: 99.4 us -> 99.2 us (level)
  no operation moved by 1% of the time
where the time goes in v5:
time: 99.2 us; the launch traced here: 98.8 us
  Pallas kernels  98.2 us (99%)
    pallas_call x1, Pallas kernels, on_device(): pl.pallas_call(functools.partial(kernel, nx, ny, nz, tuple(shapes)), out_...  95.5 us
    pallas_call x1, Pallas kernels, on_device(): pl.pallas_call(hand_over, out_shape=out_shape, in_specs=[anywhere] * 5, o...  2.75 us

profile of v5, /device:TPU:14, one launch (start us, length us, event | category | flops | bytes accessed | tf_op | source)
XLA Modules:
  0.0 98.8 jit_solution(2692254399691566536)
XLA Ops:
  0.6 95.5 %shard_map.110 = (f32[2,2048]{1,0:T(2,128)}, f32[2,8]{1,0:T(2,128)}, f32[96,2048]{1,0:T(8,128)}, f32[96,2048]{1,0:T(8,128)}, f32[96,2048]{1,0:T(8,128)}) custom-call(bf16[2,2048]{1,0:T(2,128)(2,1)} %bitcast.23, bf16[2,2048]{1,0:T(2,128)(2,1)} %bitcast.24, s32[2,8]{1,0:T(2,128)} %bitcast.25, f32[2,8]{1,0:T(2,128)} %bitcast.26, bf16[96,2048]{1,0:T(8,128)(2,1)} %bitcast.20, ...), custom_call_target="tpu_custom_call" | custom-call | tf_op jit(solution)/shard_map/pallas_call | solution.py:519
  96.1 2.7 %shard_map.111 = (f32[2,2048]{1,0:T(2,128)}, f32[2,8]{1,0:T(2,128)}, f32[96,2048]{1,0:T(8,128)}, f32[96,2048]{1,0:T(8,128)}, f32[96,2048]{1,0:T(8,128)}) custom-call(f32[2,2048]{1,0:T(2,128)} %get-tuple-element.15.refs_0_, f32[2,8]{1,0:T(2,128)} %get-tuple-element.16.refs_1_, f32[96,2048]{1,0:T(8,128)} %get-tuple-element.17.refs_2_, ...), custom_call_target="tpu_custom_call" | custom-call | tf_op jit(solution)/shard_map/pallas_call | solution.py:532
